TPU v7x, 32 devices: a whole 2x2x4 slice. The times are simulated.
32 devices in a mesh: dp: 16 (over z, y, core), fsdp: 2 (over x).
Axes of the slice: x: 2, y: 2, z: 4, core: 2. Of those that a mesh axis runs over, the one named last changes fastest.
Arguments:
- inputs: bfloat16 [64, 640, 768], P(('dp', 'fsdp')), may hold values from -6 to 6
- segments: int32 [64, 640], P(('dp', 'fsdp')), may hold values from 0 to 3, as said below
- query_wordword: bfloat16 [768, 768], P('fsdp'), may hold values from -0.21875 to 0.21875
- query_wordent: bfloat16 [768, 768], P('fsdp'), may hold values from -0.21875 to 0.21875
- query_entword: bfloat16 [768, 768], P('fsdp'), may hold values from -0.21875 to 0.21875
- query_entent: bfloat16 [768, 768], P('fsdp'), may hold values from -0.21875 to 0.21875
- bias_wordword: bfloat16 [768], P('fsdp'), may hold values from -3 to 3
- bias_wordent: bfloat16 [768], P('fsdp'), may hold values from -3 to 3
- bias_entword: bfloat16 [768], P('fsdp'), may hold values from -3 to 3
- bias_entent: bfloat16 [768], P('fsdp'), may hold values from -3 to 3
- key_weight: bfloat16 [768, 768], P('fsdp'), may hold values from -0.21875 to 0.21875
- value_weight: bfloat16 [768, 768], P('fsdp'), may hold values from -0.21875 to 0.21875
- value_bias: bfloat16 [768], P('fsdp'), may hold values from -3 to 3
- out_weight: bfloat16 [768, 768], P('fsdp'), may hold values from -0.875 to 0.875
- out_bias: bfloat16 [768], P('fsdp'), may hold values from -3 to 3
- gain_attn: bfloat16 [768], P('fsdp'), may hold values from 0.099609375 to 1.8984375
- shift_attn: bfloat16 [768], P('fsdp'), may hold values from -3 to 3
- inner_weight: bfloat16 [768, 3072], P('fsdp'), may hold values from -0.21875 to 0.21875
- inner_bias: bfloat16 [3072], P('fsdp'), may hold values from -3 to 3
- down_weight: bfloat16 [3072, 768], P('fsdp'), may hold values from -0.109375 to 0.109375
- down_bias: bfloat16 [768], P('fsdp'), may hold values from -3 to 3
- gain_ffn: bfloat16 [768], P('fsdp'), may hold values from 0.099609375 to 1.8984375
- shift_ffn: bfloat16 [768], P('fsdp'), may hold values from -3 to 3
- cotangent: bfloat16 [64, 640, 768], P(('dp', 'fsdp')), may hold values from -6 to 6
Outputs:
- output: bfloat16 [64, 640, 768], P(('dp', 'fsdp'))
- grad_inputs: float32 [64, 640, 768], P(('dp', 'fsdp'))
- grad_query_wordword: float32 [768, 768], P('fsdp')
- grad_query_wordent: float32 [768, 768], P('fsdp')
- grad_query_entword: float32 [768, 768], P('fsdp')
- grad_query_entent: float32 [768, 768], P('fsdp')
- grad_bias_wordword: float32 [768], P('fsdp')
- grad_bias_wordent: float32 [768], P('fsdp')
- grad_bias_entword: float32 [768], P('fsdp')
- grad_bias_entent: float32 [768], P('fsdp')
- grad_key_weight: float32 [768, 768], P('fsdp')
- grad_value_weight: float32 [768, 768], P('fsdp')
- grad_value_bias: float32 [768], P('fsdp')
- grad_out_weight: float32 [768, 768], P('fsdp')
- grad_out_bias: float32 [768], P('fsdp')
- grad_gain_attn: float32 [768], P('fsdp')
- grad_shift_attn: float32 [768], P('fsdp')
- grad_inner_weight: float32 [768, 3072], P('fsdp')
- grad_inner_bias: float32 [3072], P('fsdp')
- grad_down_weight: float32 [3072, 768], P('fsdp')
- grad_down_bias: float32 [768], P('fsdp')
- grad_gain_ffn: float32 [768], P('fsdp')
- grad_shift_ffn: float32 [768], P('fsdp')
Inputs may be any that keep to these rules, and one draw needn't show every extreme that they name: `segments`: in each sequence the segment numbers of the 512 word rows never fall and take every value from 0 to 3; those of the 128 entity rows never fall.
All inputs are finite; a program needn't handle non-finite values.
Results may differ from a plain program's by a relative error of at most 0.02.
Values may be sent and summed in bfloat16 or wider, within the bound.
A program may use at most 256 MiB of HBM per device.

v0:
```python
import jax
import jax.numpy as jnp
from jax import lax
from jax.sharding import PartitionSpec as P

HD = 64
WORDS = 512


norm_eps = 1e-12


def dot_plain(left, right):
    return jnp.dot(left, right, preferred_element_type=jnp.float32)


def dot_rows(left, right):
    return lax.dot_general(
        left, right, (((0,), (0,)), ((), ())), preferred_element_type=jnp.float32
    )


def dot_back(left, right):
    return lax.dot_general(
        left, right, (((1,), (1,)), ((), ())), preferred_element_type=jnp.float32
    )


def column_sum(values):
    return jnp.sum(values.astype(jnp.float32), axis=0)


def norm_forward(values):
    center = values - jnp.mean(values, axis=-1, keepdims=True)
    scale = lax.rsqrt(jnp.mean(center * center, axis=-1, keepdims=True) + norm_eps)
    return (center * scale, scale)


def norm_backward(grad_normed, normed, scale):
    first = jnp.mean(grad_normed, axis=-1, keepdims=True)
    second = jnp.mean(grad_normed * normed, axis=-1, keepdims=True)
    return scale * (grad_normed - first - normed * second)


def attn_scores(wordword, wordent, entword, entent, keyset, seg_ids):
    key_words = keyset[:WORDS]
    key_ents = keyset[WORDS:]

    def product(query, keys):
        return jnp.einsum("qhd,khd->hqk", query, keys, preferred_element_type=jnp.float32)

    upper_half = jnp.concatenate([product(wordword, key_words), product(wordent, key_ents)], axis=2)
    lower_half = jnp.concatenate([product(entword, key_words), product(entent, key_ents)], axis=2)
    scores = jnp.concatenate([upper_half, lower_half], axis=1) * HD ** (-0.5)
    same = seg_ids[:, None] == seg_ids[None, :]
    return jnp.where(same[None], scores, -1000000000.0)


def attend(items):
    wordword, wordent, entword, entent, keyset, valset, seg_ids = items
    scores = attn_scores(wordword, wordent, entword, entent, keyset, seg_ids)
    peak = jnp.max(scores, axis=-1, keepdims=True)
    log_total = peak + jnp.log(jnp.sum(jnp.exp(scores - peak), axis=-1, keepdims=True))
    probs = jnp.exp(scores - log_total).astype(jnp.bfloat16)
    context = jnp.einsum("hqk,khd->qhd", probs, valset, preferred_element_type=jnp.float32)
    return (context.astype(jnp.bfloat16), log_total)


def attend_back(items):
    wordword, wordent, entword, entent, keyset, valset, seg_ids, log_total, grad_context = items
    scores = attn_scores(wordword, wordent, entword, entent, keyset, seg_ids)
    prob = jnp.exp(scores - log_total)
    grad_prob = jnp.einsum("qhd,khd->hqk", grad_context, valset, preferred_element_type=jnp.float32)
    delta = jnp.sum(prob * grad_prob, axis=-1, keepdims=True)
    grad_scores = (prob * (grad_prob - delta)).astype(jnp.bfloat16)
    grad_values = jnp.einsum(
        "hqk,qhd->khd", prob.astype(jnp.bfloat16), grad_context, preferred_element_type=jnp.float32
    ).astype(jnp.bfloat16)
    factor = HD ** (-0.5)
    key_words = keyset[:WORDS]
    key_ents = keyset[WORDS:]
    block_ww = grad_scores[:, :WORDS, :WORDS]
    block_we = grad_scores[:, :WORDS, WORDS:]
    block_ew = grad_scores[:, WORDS:, :WORDS]
    block_ee = grad_scores[:, WORDS:, WORDS:]

    def to_query(block, keys):
        return (
            jnp.einsum("hqk,khd->qhd", block, keys, preferred_element_type=jnp.float32) * factor
        ).astype(jnp.bfloat16)

    def to_key(block, query):
        return jnp.einsum("hqk,qhd->khd", block, query, preferred_element_type=jnp.float32)

    grad_key_words = (to_key(block_ww, wordword) + to_key(block_ew, entword)) * factor
    grad_key_ents = (to_key(block_we, wordent) + to_key(block_ee, entent)) * factor
    grad_keys = jnp.concatenate([grad_key_words, grad_key_ents], axis=0).astype(jnp.bfloat16)
    return (
        to_query(block_ww, key_words),
        to_query(block_we, key_ents),
        to_query(block_ew, key_words),
        to_query(block_ee, key_ents),
        grad_keys,
        grad_values,
    )


def local(
    inputs,
    segments,
    query_wordword,
    query_wordent,
    query_entword,
    query_entent,
    bias_wordword,
    bias_wordent,
    bias_entword,
    bias_entent,
    key_weight,
    value_weight,
    value_bias,
    out_weight,
    out_bias,
    gain_attn,
    shift_attn,
    inner_weight,
    inner_bias,
    down_weight,
    down_bias,
    gain_ffn,
    shift_ffn,
    cotangent,
):
    gathered = (
        lax.all_gather(query_wordword, "fsdp", axis=0, tiled=True),
        lax.all_gather(query_wordent, "fsdp", axis=0, tiled=True),
        lax.all_gather(query_entword, "fsdp", axis=0, tiled=True),
        lax.all_gather(query_entent, "fsdp", axis=0, tiled=True),
        lax.all_gather(bias_wordword, "fsdp", axis=0, tiled=True),
        lax.all_gather(bias_wordent, "fsdp", axis=0, tiled=True),
        lax.all_gather(bias_entword, "fsdp", axis=0, tiled=True),
        lax.all_gather(bias_entent, "fsdp", axis=0, tiled=True),
        lax.all_gather(key_weight, "fsdp", axis=0, tiled=True),
        lax.all_gather(value_weight, "fsdp", axis=0, tiled=True),
        lax.all_gather(value_bias, "fsdp", axis=0, tiled=True),
        lax.all_gather(out_weight, "fsdp", axis=0, tiled=True),
        lax.all_gather(out_bias, "fsdp", axis=0, tiled=True),
        lax.all_gather(gain_attn, "fsdp", axis=0, tiled=True),
        lax.all_gather(shift_attn, "fsdp", axis=0, tiled=True),
        lax.all_gather(inner_weight, "fsdp", axis=0, tiled=True),
        lax.all_gather(inner_bias, "fsdp", axis=0, tiled=True),
        lax.all_gather(down_weight, "fsdp", axis=0, tiled=True),
        lax.all_gather(down_bias, "fsdp", axis=0, tiled=True),
        lax.all_gather(gain_ffn, "fsdp", axis=0, tiled=True),
        lax.all_gather(shift_ffn, "fsdp", axis=0, tiled=True),
    )
    seqs = inputs.shape[0]
    length = inputs.shape[1]
    width = inputs.shape[2]
    ents = length - WORDS
    heads = width // HD
    word_rows = inputs[:, :WORDS].reshape(seqs * WORDS, width)
    ent_rows = inputs[:, WORDS:].reshape(seqs * ents, width)
    all_rows = inputs.reshape(seqs * length, width)

    def project(source, weight, bias, count):
        total = dot_plain(source, weight) + bias.astype(jnp.float32)
        return total.astype(jnp.bfloat16).reshape(seqs, count, heads, HD)

    wordword = project(word_rows, gathered[0], gathered[4], WORDS)
    wordent = project(word_rows, gathered[1], gathered[5], WORDS)
    entword = project(ent_rows, gathered[2], gathered[6], ents)
    entent = project(ent_rows, gathered[3], gathered[7], ents)
    keyset = dot_plain(all_rows, gathered[8]).astype(jnp.bfloat16).reshape(seqs, length, heads, HD)
    valset = project(all_rows, gathered[9], gathered[10], length)
    context, log_total = lax.map(
        attend, (wordword, wordent, entword, entent, keyset, valset, segments)
    )
    context_rows = context.reshape(seqs * length, width)
    attended = dot_plain(context_rows, gathered[11]) + gathered[12].astype(jnp.float32)
    normed_attn, scale_attn = norm_forward(all_rows.astype(jnp.float32) + attended)
    hidden = normed_attn * gathered[13].astype(jnp.float32) + gathered[14].astype(jnp.float32)
    hidden_low = hidden.astype(jnp.bfloat16)
    upper = dot_plain(hidden_low, gathered[15]) + gathered[16].astype(jnp.float32)
    active = jax.nn.gelu(upper, approximate=False).astype(jnp.bfloat16)
    fed = dot_plain(active, gathered[17]) + gathered[18].astype(jnp.float32)
    normed_ffn, scale_ffn = norm_forward(hidden + fed)
    result = normed_ffn * gathered[19].astype(jnp.float32) + gathered[20].astype(jnp.float32)
    output = result.astype(jnp.bfloat16).reshape(seqs, length, width)
    params = (
        lax.all_gather(query_wordword, "fsdp", axis=0, tiled=True),
        lax.all_gather(query_wordent, "fsdp", axis=0, tiled=True),
        lax.all_gather(query_entword, "fsdp", axis=0, tiled=True),
        lax.all_gather(query_entent, "fsdp", axis=0, tiled=True),
        lax.all_gather(bias_wordword, "fsdp", axis=0, tiled=True),
        lax.all_gather(bias_wordent, "fsdp", axis=0, tiled=True),
        lax.all_gather(bias_entword, "fsdp", axis=0, tiled=True),
        lax.all_gather(bias_entent, "fsdp", axis=0, tiled=True),
        lax.all_gather(key_weight, "fsdp", axis=0, tiled=True),
        lax.all_gather(value_weight, "fsdp", axis=0, tiled=True),
        lax.all_gather(value_bias, "fsdp", axis=0, tiled=True),
        lax.all_gather(out_weight, "fsdp", axis=0, tiled=True),
        lax.all_gather(out_bias, "fsdp", axis=0, tiled=True),
        lax.all_gather(gain_attn, "fsdp", axis=0, tiled=True),
        lax.all_gather(shift_attn, "fsdp", axis=0, tiled=True),
        lax.all_gather(inner_weight, "fsdp", axis=0, tiled=True),
        lax.all_gather(inner_bias, "fsdp", axis=0, tiled=True),
        lax.all_gather(down_weight, "fsdp", axis=0, tiled=True),
        lax.all_gather(down_bias, "fsdp", axis=0, tiled=True),
        lax.all_gather(gain_ffn, "fsdp", axis=0, tiled=True),
        lax.all_gather(shift_ffn, "fsdp", axis=0, tiled=True),
    )
    grad_out = cotangent.reshape(seqs * length, width).astype(jnp.float32)
    grad_gain_ffn = jnp.sum(grad_out * normed_ffn, axis=0)
    grad_shift_ffn = jnp.sum(grad_out, axis=0)
    grad_sum = norm_backward(grad_out * params[19].astype(jnp.float32), normed_ffn, scale_ffn)
    grad_fed = grad_sum.astype(jnp.bfloat16)
    grad_down_bias = column_sum(grad_fed)
    grad_down_weight = dot_rows(active, grad_fed)
    grad_active = dot_back(grad_fed, params[17])
    _, gelu_pull = jax.vjp(lambda inner: jax.nn.gelu(inner, approximate=False), upper)
    grad_upper = gelu_pull(grad_active)[0].astype(jnp.bfloat16)
    grad_inner_bias = column_sum(grad_upper)
    grad_inner_weight = dot_rows(hidden_low, grad_upper)
    grad_hidden = grad_sum + dot_back(grad_upper, params[15])
    grad_gain_attn = jnp.sum(grad_hidden * normed_attn, axis=0)
    grad_shift_attn = jnp.sum(grad_hidden, axis=0)
    grad_pre = norm_backward(grad_hidden * params[13].astype(jnp.float32), normed_attn, scale_attn)
    grad_attended = grad_pre.astype(jnp.bfloat16)
    grad_out_bias = column_sum(grad_attended)
    grad_out_weight = dot_rows(context_rows, grad_attended)
    grad_context = (
        dot_back(grad_attended, params[11]).astype(jnp.bfloat16).reshape(seqs, length, heads, HD)
    )
    back_items = (
        wordword,
        wordent,
        entword,
        entent,
        keyset,
        valset,
        segments,
        log_total,
        grad_context,
    )
    grad_ww, grad_we, grad_ew, grad_ee, grad_keys, grad_values = lax.map(attend_back, back_items)
    grad_ww = grad_ww.reshape(seqs * WORDS, width)
    grad_we = grad_we.reshape(seqs * WORDS, width)
    grad_ew = grad_ew.reshape(seqs * ents, width)
    grad_ee = grad_ee.reshape(seqs * ents, width)
    grad_keys = grad_keys.reshape(seqs * length, width)
    grad_values = grad_values.reshape(seqs * length, width)
    grad_query_wordword = dot_rows(word_rows, grad_ww)
    grad_query_wordent = dot_rows(word_rows, grad_we)
    grad_query_entword = dot_rows(ent_rows, grad_ew)
    grad_query_entent = dot_rows(ent_rows, grad_ee)
    grad_key_weight = dot_rows(all_rows, grad_keys)
    grad_value_weight = dot_rows(all_rows, grad_values)
    word_back = dot_back(grad_ww, params[0]) + dot_back(grad_we, params[1])
    ent_back = dot_back(grad_ew, params[2]) + dot_back(grad_ee, params[3])
    query_back = jnp.concatenate(
        [word_back.reshape(seqs, WORDS, width), ent_back.reshape(seqs, ents, width)], axis=1
    )
    grad_inputs = (
        grad_pre
        + query_back.reshape(seqs * length, width)
        + dot_back(grad_keys, params[8])
        + dot_back(grad_values, params[9])
    ).reshape(seqs, length, width)
    shares = (
        lax.psum_scatter(
            grad_query_wordword.astype(jnp.bfloat16), "fsdp", scatter_dimension=0, tiled=True
        ).astype(jnp.float32),
        lax.psum_scatter(
            grad_query_wordent.astype(jnp.bfloat16), "fsdp", scatter_dimension=0, tiled=True
        ).astype(jnp.float32),
        lax.psum_scatter(
            grad_query_entword.astype(jnp.bfloat16), "fsdp", scatter_dimension=0, tiled=True
        ).astype(jnp.float32),
        lax.psum_scatter(
            grad_query_entent.astype(jnp.bfloat16), "fsdp", scatter_dimension=0, tiled=True
        ).astype(jnp.float32),
        lax.psum_scatter(
            column_sum(grad_ww).astype(jnp.bfloat16), "fsdp", scatter_dimension=0, tiled=True
        ).astype(jnp.float32),
        lax.psum_scatter(
            column_sum(grad_we).astype(jnp.bfloat16), "fsdp", scatter_dimension=0, tiled=True
        ).astype(jnp.float32),
        lax.psum_scatter(
            column_sum(grad_ew).astype(jnp.bfloat16), "fsdp", scatter_dimension=0, tiled=True
        ).astype(jnp.float32),
        lax.psum_scatter(
            column_sum(grad_ee).astype(jnp.bfloat16), "fsdp", scatter_dimension=0, tiled=True
        ).astype(jnp.float32),
        lax.psum_scatter(
            grad_key_weight.astype(jnp.bfloat16), "fsdp", scatter_dimension=0, tiled=True
        ).astype(jnp.float32),
        lax.psum_scatter(
            grad_value_weight.astype(jnp.bfloat16), "fsdp", scatter_dimension=0, tiled=True
        ).astype(jnp.float32),
        lax.psum_scatter(
            column_sum(grad_values).astype(jnp.bfloat16), "fsdp", scatter_dimension=0, tiled=True
        ).astype(jnp.float32),
        lax.psum_scatter(
            grad_out_weight.astype(jnp.bfloat16), "fsdp", scatter_dimension=0, tiled=True
        ).astype(jnp.float32),
        lax.psum_scatter(
            grad_out_bias.astype(jnp.bfloat16), "fsdp", scatter_dimension=0, tiled=True
        ).astype(jnp.float32),
        lax.psum_scatter(
            grad_gain_attn.astype(jnp.bfloat16), "fsdp", scatter_dimension=0, tiled=True
        ).astype(jnp.float32),
        lax.psum_scatter(
            grad_shift_attn.astype(jnp.bfloat16), "fsdp", scatter_dimension=0, tiled=True
        ).astype(jnp.float32),
        lax.psum_scatter(
            grad_inner_weight.astype(jnp.bfloat16), "fsdp", scatter_dimension=0, tiled=True
        ).astype(jnp.float32),
        lax.psum_scatter(
            grad_inner_bias.astype(jnp.bfloat16), "fsdp", scatter_dimension=0, tiled=True
        ).astype(jnp.float32),
        lax.psum_scatter(
            grad_down_weight.astype(jnp.bfloat16), "fsdp", scatter_dimension=0, tiled=True
        ).astype(jnp.float32),
        lax.psum_scatter(
            grad_down_bias.astype(jnp.bfloat16), "fsdp", scatter_dimension=0, tiled=True
        ).astype(jnp.float32),
        lax.psum_scatter(
            grad_gain_ffn.astype(jnp.bfloat16), "fsdp", scatter_dimension=0, tiled=True
        ).astype(jnp.float32),
        lax.psum_scatter(
            grad_shift_ffn.astype(jnp.bfloat16), "fsdp", scatter_dimension=0, tiled=True
        ).astype(jnp.float32),
    )
    summed = (
        lax.psum(shares[0].astype(jnp.bfloat16), "dp").astype(jnp.float32),
        lax.psum(shares[1].astype(jnp.bfloat16), "dp").astype(jnp.float32),
        lax.psum(shares[2].astype(jnp.bfloat16), "dp").astype(jnp.float32),
        lax.psum(shares[3].astype(jnp.bfloat16), "dp").astype(jnp.float32),
        lax.psum(shares[4].astype(jnp.bfloat16), "dp").astype(jnp.float32),
        lax.psum(shares[5].astype(jnp.bfloat16), "dp").astype(jnp.float32),
        lax.psum(shares[6].astype(jnp.bfloat16), "dp").astype(jnp.float32),
        lax.psum(shares[7].astype(jnp.bfloat16), "dp").astype(jnp.float32),
        lax.psum(shares[8].astype(jnp.bfloat16), "dp").astype(jnp.float32),
        lax.psum(shares[9].astype(jnp.bfloat16), "dp").astype(jnp.float32),
        lax.psum(shares[10].astype(jnp.bfloat16), "dp").astype(jnp.float32),
        lax.psum(shares[11].astype(jnp.bfloat16), "dp").astype(jnp.float32),
        lax.psum(shares[12].astype(jnp.bfloat16), "dp").astype(jnp.float32),
        lax.psum(shares[13].astype(jnp.bfloat16), "dp").astype(jnp.float32),
        lax.psum(shares[14].astype(jnp.bfloat16), "dp").astype(jnp.float32),
        lax.psum(shares[15].astype(jnp.bfloat16), "dp").astype(jnp.float32),
        lax.psum(shares[16].astype(jnp.bfloat16), "dp").astype(jnp.float32),
        lax.psum(shares[17].astype(jnp.bfloat16), "dp").astype(jnp.float32),
        lax.psum(shares[18].astype(jnp.bfloat16), "dp").astype(jnp.float32),
        lax.psum(shares[19].astype(jnp.bfloat16), "dp").astype(jnp.float32),
        lax.psum(shares[20].astype(jnp.bfloat16), "dp").astype(jnp.float32),
    )
    return (
        output,
        grad_inputs,
        summed[0],
        summed[1],
        summed[2],
        summed[3],
        summed[4],
        summed[5],
        summed[6],
        summed[7],
        summed[8],
        summed[9],
        summed[10],
        summed[11],
        summed[12],
        summed[13],
        summed[14],
        summed[15],
        summed[16],
        summed[17],
        summed[18],
        summed[19],
        summed[20],
    )


def solution(mesh):
    placed = (
        P(("dp", "fsdp"), None, None),
        P(("dp", "fsdp"), None),
        P("fsdp", None),
        P("fsdp", None),
        P("fsdp", None),
        P("fsdp", None),
        P("fsdp"),
        P("fsdp"),
        P("fsdp"),
        P("fsdp"),
        P("fsdp", None),
        P("fsdp", None),
        P("fsdp"),
        P("fsdp", None),
        P("fsdp"),
        P("fsdp"),
        P("fsdp"),
        P("fsdp", None),
        P("fsdp"),
        P("fsdp", None),
        P("fsdp"),
        P("fsdp"),
        P("fsdp"),
        P(("dp", "fsdp"), None, None),
    )
    return jax.shard_map(
        local,
        mesh=mesh,
        in_specs=placed,
        out_specs=(
            P(("dp", "fsdp"), None, None),
            P(("dp", "fsdp"), None, None),
            P("fsdp", None),
            P("fsdp", None),
            P("fsdp", None),
            P("fsdp", None),
            P("fsdp"),
            P("fsdp"),
            P("fsdp"),
            P("fsdp"),
            P("fsdp", None),
            P("fsdp", None),
            P("fsdp"),
            P("fsdp", None),
            P("fsdp"),
            P("fsdp"),
            P("fsdp"),
            P("fsdp", None),
            P("fsdp"),
            P("fsdp", None),
            P("fsdp"),
            P("fsdp"),
            P("fsdp"),
        ),
        check_vma=False,
    )
```

profile of v0, /device:TPU:1, one launch (start us, length us, event | category | flops | bytes accessed | tf_op | source)
XLA Modules:
  0.0 1033.6 jit_solution(2034211060447915402)
XLA Ops:
  17.1 3.8 all-gather
  21.5 4.0 all-gather.1
  53.0 3.8 all-gather.8
  71.4 4.9 add_convert_fusion.2
  84.3 4.2 convolution_convert_fusion.3
  95.3 3.8 add_convert_fusion.4
  107.4 4.3 add_convert_fusion.3
  118.8 12.8 %all-gather.30.cloned.1.call-done = bf16[768,768]{1,0:T(8,128)(2,1)} async-done(((bf16[384,768]{1,0:T(8,128)(2,1)}), bf16[768,768]{1,0:T(8,128)(2,1)}) %all-gather.30.cloned.1.call-update) | async-done | bytes 1179664 | tf_op jit(solution)/shard_map/all_gather | solution.py:137
  133.8 21.9 %all-gather.32.cloned.1.call-done = bf16[768,768]{1,0:T(8,128)(2,1)} async-done(((bf16[384,768]{1,0:T(8,128)(2,1)}), bf16[768,768]{1,0:T(8,128)(2,1)}) %all-gather.32.cloned.1.call-update) | async-done | bytes 1179664 | tf_op jit(solution)/shard_map/all_gather | solution.py:138
  160.1 77.2 %while.32 = (s32[]{:T(128)}, bf16[2,640,12,64]{1,3,2,0:T(8,128)(2,1)}, f32[2,12,640,1]{2,1,3,0:T(8,128)}, bf16[2,640,12,64]{1,3,2,0:T(8,128)(2,1)}, s32[2,640]{1...) while((s32[]{:T(128)}, ...), condition=%wide.region_3.4_spmd, body=%wide.region_0.3_spmd.sunk | while | flops 1357488640 | bytes 143594256 | solution.py:176
  176.8 7.3 fusion.314
  184.1 9.0 exponential_reduce_fusion.2
  194.4 9.4 fusion.315
  210.6 7.3 fusion.314
  217.8 9.0 exponential_reduce_fusion.2
  228.2 9.1 fusion.315
  237.3 4.4 copy.147
  243.4 4.5 fusion.207
  250.5 47.1 %multiply_convert_fusion.4 = (bf16[1280,3072]{1,0:T(8,128)(2,1)}, f32[1280,3072]{1,0:T(8,128)}, f32[1280,3072]{1,0:T(8,128)}) fusion(f32[3072]{0:T(1024)S(1)} %bitcast.387, bf16[768,3072]{1,0:T(8,128)(2,1)} %all-gather.36.cloned.1.call-done, f32[1280,768]{1,0:T(8,128)} %copy-done.16, f32[768]{0:T(1024)S(1)} %copy-done.81, f32[768]{0:T(1024)S(1)} %copy-done.73, ...), kind=kOutput, calls=%fused_computation.138 | convolution fusion | flops 6304235520 | bytes 48001024 | tf_op jit(solution)/shard_map/dot_general | solution.py:14
  297.6 10.9 %all-gather.38.cloned.1.call-done = bf16[3072,768]{1,0:T(8,128)(2,1)} async-done(((bf16[1536,768]{1,0:T(8,128)(2,1)}), bf16[3072,768]{1,0:T(8,128)(2,1)}) %all-gather.38.cloned.1.call-update) | async-done | bytes 4718608 | tf_op jit(solution)/shard_map/all_gather | solution.py:152
  308.5 11.1 %fusion.208 = (f32[1280]{0:T(1024)S(1)}, f32[1280,768]{1,0:T(8,128)S(1)}) fusion(f32[768]{0:T(1024)S(1)} %copy-done.84, bf16[1280,3072]{1,0:T(8,128)(2,1)} %get-tuple-element.415, bf16[3072,768]{1,0:T(8,128)(2,1)} %all-gather.38.cloned.1.call-done, f32[768]{0:T(1024)S(1)} %copy-done.81, f32[768]{0:T(1024)S(1)} %copy-done.73, ...), kind=kOutput, calls=%fused_computation.242 | convolution fusion | flops 6046678016 | bytes 20471808 | tf_op jit(solution)/shard_map/dot_general | solution.py:14
  321.1 4.0 fusion.179
  328.4 23.8 %fusion.209 = (bf16[3072]{0:T(1024)(128)(2,1)}, bf16[1280,3072]{1,0:T(8,128)(2,1)}) fusion(f32[1280,3072]{1,0:T(8,128)} %get-tuple-element.416, bf16[3072,768]{1,0:T(8,128)(2,1)} %all-gather.38.cloned.1.call-done, f32[1280,768]{1,0:T(8,128)} %get-tuple-element.412, f32[1280,3072]{1,0:T(8,128)} %get-tuple-element.420, f32[3072]{0:T(1024)S(1)} %bitcast.388), kind=kOutput, calls=%fused_computation.243 | convolution fusion | flops 6103692288 | bytes 47990784 | tf_op jit(solution)/shard_map/dot_general | solution.py:24
  352.2 13.4 %multiply_reduce_fusion.1 = (bf16[768]{0:T(1024)(128)(2,1)}, f32[1280]{0:T(1024)S(1)}, f32[1280]{0:T(1024)S(1)}, bf16[768]{0:T(1024)(128)(2,1)}, f32[1280,768]{1,0:T(8,128)S(1)}) fusion(f32[1280,768]{1,0:T(8,128)} %copy-done.16, f32[1280]{0:T(1024)S(1)} %add_rsqrt_fusion.1, f32[1280]{0:T(1024)S(1)} %broadcast_multiply_fusion.4, f32[768]{0:T(1024)S(1)} %copy-done.73, ...), kind=kOutput, calls=%fused_computation.168 | convolution fusion | flops 6049624064 | bytes 24406016 | tf_op jit(solution)/shard_map/dot_general | solution.py:24
  383.8 139.2 %while.33 = (s32[]{:T(128)}, bf16[2,512,12,64]{1,3,2,0:T(8,128)(2,1)}, bf16[2,512,12,64]{1,3,2,0:T(8,128)(2,1)}, bf16[2,128,12,64]{1,3,2,0:T(8,128)(2,1)}, bf16[...) while((s32[]{:T(128)}, ...), condition=%wide.region_14.15_spmd, body=%wide.region_12.14_spmd.sunk | while | flops 3894239232 | bytes 225811664 | solution.py:246
  389.8 6.4 fusion.343
  400.8 25.9 %multiply_convert_fusion.6 = bf16[12,640,640]{1,2,0:T(8,128)(2,1)} fusion(bf16[2,640,12,64]{1,3,2,0:T(8,128)(2,1)} %get-tuple-element.682, s32[]{:T(128)} %get-tuple-element.648, bf16[2,640,12,64]{1,3,2,0:T(8,128)(2,1)} %get-tuple-element.681, f32[12,640]{1,0:T(8,128)} %dynamic-slice_bitcast_fusion.42, f32[12,128,128]{1,2,0:T(8,128)} %fusion.340, ...), kind=kOutput, calls=%fused_computation.40.clone.1 | convolution fusion | flops 1336942720 | bytes 53987328 | tf_op jit(solution)/shard_map/while/body/eval_jaxpr/sub | solution.py:75
  426.8 5.0 fusion.351
  443.5 10.2 fusion.353
  459.2 6.4 fusion.343
  470.2 25.8 %multiply_convert_fusion.6 = bf16[12,640,640]{1,2,0:T(8,128)(2,1)} fusion(bf16[2,640,12,64]{1,3,2,0:T(8,128)(2,1)} %get-tuple-element.682, s32[]{:T(128)} %get-tuple-element.648, bf16[2,640,12,64]{1,3,2,0:T(8,128)(2,1)} %get-tuple-element.681, f32[12,640]{1,0:T(8,128)} %dynamic-slice_bitcast_fusion.42, f32[12,128,128]{1,2,0:T(8,128)} %fusion.340, ...), kind=kOutput, calls=%fused_computation.40.clone.1 | convolution fusion | flops 1336942720 | bytes 53987328 | tf_op jit(solution)/shard_map/while/body/eval_jaxpr/sub | solution.py:75
  496.0 5.0 fusion.351
  512.7 10.2 fusion.353
  563.0 5.2 convolution_convert_fusion.4
  568.3 12.2 %convolution_convert_fusion.1 = bf16[768,3072]{1,0:T(8,128)(2,1)} fusion(bf16[1280,3072]{1,0:T(8,128)(2,1)} %get-tuple-element.425, f32[1280,768]{1,0:T(8,128)} %copy-done.16, f32[768]{0:T(1024)S(1)} %copy-done.82, f32[768]{0:T(1024)S(1)} %copy-done.74, f32[1280]{0:T(1024)S(1)} %copy-done.71, f32[1280]{0:T(1024)S(1)} %copy-done.67), kind=kOutput, calls=%fused_computation.153 | convolution fusion | flops 6047072256 | bytes 16531456 | tf_op jit(solution)/shard_map/dot_general | solution.py:18
  581.0 11.3 %convolution_convert_fusion = bf16[3072,768]{1,0:T(8,128)(2,1)} fusion(bf16[1280,3072]{1,0:T(8,128)(2,1)} %get-tuple-element.415, f32[1280,768]{1,0:T(8,128)} %get-tuple-element.412), kind=kOutput, calls=%fused_computation.152 | convolution fusion | flops 6043140096 | bytes 16515072 | tf_op jit(solution)/shard_map/dot_general | solution.py:18
  596.7 7.3 reduce-scatter.36.cloned.1.call-done
  606.1 22.6 %reduce-scatter.38.cloned.1.call-done = bf16[384,768]{1,0:T(8,128)(2,1)} async-done(((bf16[768,768]{1,0:T(8,128)(2,1)}), bf16[384,768]{1,0:T(8,128)(2,1)}) %reduce-scatter.38.cloned.1.call-update) | async-done | bytes 589840
  630.8 22.4 %reduce-scatter.32.cloned.1.call-done = bf16[384,768]{1,0:T(8,128)(2,1)} async-done(((bf16[768,768]{1,0:T(8,128)(2,1)}), bf16[384,768]{1,0:T(8,128)(2,1)}) %reduce-scatter.32.cloned.1.call-update) | async-done | bytes 589840
  655.4 22.4 %reduce-scatter.34.cloned.1.call-done = bf16[384,768]{1,0:T(8,128)(2,1)} async-done(((bf16[768,768]{1,0:T(8,128)(2,1)}), bf16[384,768]{1,0:T(8,128)(2,1)}) %reduce-scatter.34.cloned.1.call-update) | async-done | bytes 589840
  679.9 22.4 %reduce-scatter.22.cloned.1.call-done = bf16[384,768]{1,0:T(8,128)(2,1)} async-done(((bf16[768,768]{1,0:T(8,128)(2,1)}), bf16[384,768]{1,0:T(8,128)(2,1)}) %reduce-scatter.22.cloned.1.call-update) | async-done | bytes 589840 | tf_op jit(solution)/shard_map/reduce_scatter | solution.py:304
  702.3 62.8 %reduce-scatter.24.cloned.1.call-done = bf16[384,3072]{1,0:T(8,128)(2,1)} async-done(((bf16[768,3072]{1,0:T(8,128)(2,1)}), bf16[384,3072]{1,0:T(8,128)(2,1)}) %reduce-scatter.24.cloned.1.call-update) | async-done | bytes 2359312 | tf_op jit(solution)/shard_map/reduce_scatter | solution.py:316
  765.2 62.8 %reduce-scatter.26.cloned.1.call-done = bf16[1536,768]{1,0:T(8,128)(2,1)} async-done(((bf16[3072,768]{1,0:T(8,128)(2,1)}), bf16[1536,768]{1,0:T(8,128)(2,1)}) %reduce-scatter.26.cloned.1.call-update) | async-done | bytes 2359312 | tf_op jit(solution)/shard_map/reduce_scatter | solution.py:322
  837.6 6.6 all-reduce.14
  845.2 60.0 %all-reduce.12 = (bf16[384]{0:T(512)(128)(2,1)S(1)}, bf16[384]{0:T(512)(128)(2,1)S(1)}, bf16[384]{0:T(512)(128)(2,1)S(1)}, bf16[384]{0:T(512)(128)(2,1)S(1)}, bf...) all-reduce(bf16[384]{0:T(512)(128)(2,1)S(1)} %dynamic-slice.1, ...), channel_id=1, replica_groups=mesh['dp'=16,'fsdp'=2] {'dp'}, use_global_device_ids=true, to_apply=%region_25.26 | all-reduce | flops 5760 | bytes 23040 | tf_op jit(solution)/shard_map/psum | solution.py:340
  924.0 3.9 fusion.172
  927.9 83.0 %all-reduce.17.cloned.1.call-done = (bf16[384,768]{0,1:T(8,128)(2,1)}, bf16[384,768]{0,1:T(8,128)(2,1)}, bf16[384,768]{0,1:T(8,128)(2,1)}, bf16[384,768]{0,1:T(8...) async-done(((bf16[384,768]{0,1:T(8,128)(2,1)}, ...) | async-done | bytes 8847376 | tf_op jit(solution)/shard_map/psum | solution.py:336
  1011.0 4.6 convert_element_type.378
  (490 shorter events, 267.9 us)
Async XLA Ops:
  7.2 64.2 %all-gather.22.cloned.1.call-start = ((), (), s32[]{:S(2)}) async-start(), calls=%async_computation.9 | async-start | bytes 1769472 | tf_op jit(solution)/shard_map/all_gather | solution.py:144
  7.9 76.4 %all-gather.26.cloned.1.call-start = ((), (), s32[]{:S(2)}) async-start(), calls=%async_computation.11 | async-start | bytes 1769472 | tf_op jit(solution)/shard_map/all_gather | solution.py:143
  8.7 86.6 %all-gather.24.cloned.1.call-start = ((), (), s32[]{:S(2)}) async-start(), calls=%async_computation.10 | async-start | bytes 1769472 | tf_op jit(solution)/shard_map/all_gather | solution.py:135
  9.4 98.0 %all-gather.28.cloned.1.call-start = ((), (), s32[]{:S(2)}) async-start(), calls=%async_computation.12 | async-start | bytes 1769472 | tf_op jit(solution)/shard_map/all_gather | solution.py:136
  10.0 121.6 %all-gather.30.cloned.1.call-start = ((), (), s32[]{:S(2)}) async-start(), calls=%async_computation.13 | async-start | bytes 1769472 | tf_op jit(solution)/shard_map/all_gather | solution.py:137
  10.6 145.2 %all-gather.32.cloned.1.call-start = ((), (), s32[]{:S(2)}) async-start(), calls=%async_computation.14 | async-start | bytes 1769472 | tf_op jit(solution)/shard_map/all_gather | solution.py:138
  11.2 232.2 %all-gather.34.cloned.1.call-start = ((), (), s32[]{:S(2)}) async-start(), calls=%async_computation.15 | async-start | bytes 1769472 | tf_op jit(solution)/shard_map/all_gather | solution.py:146
  11.9 9.6 copy-start.89
  11.9 14.2 %copy-start.90 = (bf16[384]{0:T(512)(128)(2,1)S(1)}, bf16[384]{0:T(512)(128)(2,1)}, u32[]{:S(2)}) copy-start(bf16[384]{0:T(512)(128)(2,1)} %param.35) | copy-start | bytes 2308
  11.9 41.1 %copy-start.87 = (bf16[1536]{0:T(1024)(128)(2,1)S(1)}, bf16[1536]{0:T(1024)(128)(2,1)}, u32[]{:S(2)}) copy-start(bf16[1536]{0:T(1024)(128)(2,1)} %param.46) | copy-start | bytes 9220
  11.9 58.4 %copy-start.6 = (bf16[2,640,768]{2,1,0:T(8,128)(2,1)S(1)}, bf16[2,640,768]{2,1,0:T(8,128)(2,1)}, u32[]{:S(2)}) copy-start(bf16[2,640,768]{2,1,0:T(8,128)(2,1)} %param.51) | copy-start | bytes 5898244
  12.0 238.5 %all-gather.36.cloned.1.call-start = ((), (), s32[]{:S(2)}) async-start(), calls=%async_computation.16 | async-start | bytes 7077888 | tf_op jit(solution)/shard_map/all_gather | solution.py:150
  12.7 295.8 %all-gather.38.cloned.1.call-start = ((), (), s32[]{:S(2)}) async-start(), calls=%async_computation.17 | async-start | bytes 7077888 | tf_op jit(solution)/shard_map/all_gather | solution.py:152
  13.4 579.0 %reduce-scatter.28.cloned.1.call-start = ((), (), s32[]{:S(2)}) async-start(), calls=%async_computation.21 | async-start | bytes 1769472
  15.0 80.2 %copy-start.43 = (bf16[2,512,768]{2,1,0:T(8,128)(2,1)}, bf16[2,512,768]{2,1,0:T(8,128)(2,1)S(1)}, u32[]{:S(2)}) copy-start(bf16[2,512,768]{2,1,0:T(8,128)(2,1)S(1)} %slice.44) | copy-start | bytes 4718596
  65.8 10.5 %copy-start.68 = (f32[768]{0:T(1024)}, f32[768]{0:T(1024)S(1)}, u32[]{:S(2)}) copy-start(f32[768]{0:T(1024)S(1)} %reshape.363) | copy-start | bytes 9220
  115.7 40.0 %copy-start.34 = (bf16[2,128,768]{2,1,0:T(8,128)(2,1)S(1)}, bf16[2,128,768]{2,1,0:T(8,128)(2,1)}, u32[]{:S(2)}) copy-start(bf16[2,128,768]{2,1,0:T(8,128)(2,1)} %slice.45) | copy-start | bytes 1179652
  115.7 40.0 %copy-start.85 = (f32[768]{0:T(1024)S(1)}, f32[768]{0:T(1024)}, u32[]{:S(2)}) copy-start(f32[768]{0:T(1024)} %reshape.357) | copy-start | bytes 9220
  175.0 9.0 copy-start
  184.0 9.1 copy-start.63
  208.8 9.0 copy-start
  217.8 9.1 copy-start.63
  248.0 117.7 %copy-start.66 = (f32[1280]{0:T(1024)}, f32[1280]{0:T(1024)S(1)}, u32[]{:S(2)}) copy-start(f32[1280]{0:T(1024)S(1)} %broadcast_multiply_fusion.4) | copy-start | bytes 15364
  250.4 115.2 %copy-start.70 = (f32[1280]{0:T(1024)}, f32[1280]{0:T(1024)S(1)}, u32[]{:S(2)}) copy-start(f32[1280]{0:T(1024)S(1)} %add_rsqrt_fusion.1) | copy-start | bytes 15364
  250.5 58.0 %copy-start.84 = (f32[768]{0:T(1024)S(1)}, f32[768]{0:T(1024)}, u32[]{:S(2)}) copy-start(f32[768]{0:T(1024)} %reshape.362) | copy-start | bytes 9220
  352.2 13.4 %copy-start.17 = (f32[1280,768]{1,0:T(8,128)S(1)}, f32[1280,768]{1,0:T(8,128)}, u32[]{:S(2)}) copy-start(f32[1280,768]{1,0:T(8,128)} %copy-done.16) | copy-start | bytes 11796484
  377.3 6.5 copy-start.3
  377.3 6.5 copy-start.5
  389.8 6.4 copy-start.10
  426.8 7.4 copy-start.1
  496.0 7.4 copy-start.1
  532.8 61.8 %reduce-scatter.30.cloned.1.call-start = ((), (), s32[]{:S(2)}) async-start(), calls=%async_computation.22 | async-start | bytes 1769472
  541.1 62.9 %reduce-scatter.36.cloned.1.call-start = ((), (), s32[]{:S(2)}) async-start(), calls=%async_computation.25 | async-start | bytes 1769472
  548.0 80.7 %reduce-scatter.38.cloned.1.call-start = ((), (), s32[]{:S(2)}) async-start(), calls=%async_computation.26 | async-start | bytes 1769472
  555.4 97.8 %reduce-scatter.32.cloned.1.call-start = ((), (), s32[]{:S(2)}) async-start(), calls=%async_computation.23 | async-start | bytes 1769472
  558.6 119.2 %reduce-scatter.34.cloned.1.call-start = ((), (), s32[]{:S(2)}) async-start(), calls=%async_computation.24 | async-start | bytes 1769472
  562.9 139.4 %reduce-scatter.22.cloned.1.call-start = ((), (), s32[]{:S(2)}) async-start(), calls=%async_computation.18 | async-start | bytes 1769472 | tf_op jit(solution)/shard_map/reduce_scatter | solution.py:304
  568.2 196.9 %reduce-scatter.24.cloned.1.call-start = ((), (), s32[]{:S(2)}) async-start(), calls=%async_computation.19 | async-start | bytes 7077888 | tf_op jit(solution)/shard_map/reduce_scatter | solution.py:316
  580.5 247.5 %reduce-scatter.26.cloned.1.call-start = ((), (), s32[]{:S(2)}) async-start(), calls=%async_computation.20 | async-start | bytes 7077888 | tf_op jit(solution)/shard_map/reduce_scatter | solution.py:322
  592.3 418.6 %all-reduce.17.cloned.1.call-start = ((), (), s32[]{:S(2)}) async-start(), calls=%async_computation.27 | async-start | bytes 17694720 | tf_op jit(solution)/shard_map/psum | solution.py:336
  829.5 8.1 copy-start.77
  829.5 8.1 copy-start.78
  829.6 8.1 copy-start.79
  830.5 6.7 copy-start.13
  832.7 79.4 %copy-start.31 = (bf16[2,128,12,64]{1,0,3,2:T(2,128)(2,1)S(1)}, bf16[2,128,12,64]{1,0,3,2:T(2,128)(2,1)}, u32[]{:S(2)}) copy-start(bf16[2,128,12,64]{1,0,3,2:T(2,128)(2,1)} %copy-done.30) | copy-start | bytes 1179652
  832.7 81.2 %copy-start.33 = (bf16[2,128,12,64]{1,0,3,2:T(2,128)(2,1)S(1)}, bf16[2,128,12,64]{1,0,3,2:T(2,128)(2,1)}, u32[]{:S(2)}) copy-start(bf16[2,128,12,64]{1,0,3,2:T(2,128)(2,1)} %copy-done.32) | copy-start | bytes 1179652
  837.5 78.2 %copy-start.46 = (bf16[96,8,2,512]{3,1,2,0:T(8,128)(2,1)S(1)}, bf16[96,8,2,512]{3,1,2,0:T(8,128)(2,1)}, u32[]{:S(2)}) copy-start(bf16[96,8,2,512]{3,1,2,0:T(8,128)(2,1)} %copy-done.45) | copy-start | bytes 4718596
  905.2 10.6 %copy-start.92 = (bf16[768,768]{1,0:T(8,128)(2,1)S(1)}, bf16[768,768]{1,0:T(8,128)(2,1)}, u32[]{:S(2)}) copy-start(bf16[768,768]{1,0:T(8,128)(2,1)} %all-gather.24.cloned.1.call-done) | copy-start | bytes 3538948
  (87 other events, 261.1 us)
Sparse Core Ops, SparseCore 0:
  9.5 24.7 all-gather.21
  35.9 22.8 all-gather.25
  60.3 22.7 all-gather.23
  84.6 22.7 all-gather.27
  108.8 22.7 all-gather.29
  132.9 22.7 all-gather.31
  157.3 22.7 all-gather.33
  181.6 62.6 all-gather.35
  245.8 62.6 all-gather.37
  532.9 21.8 reduce-scatter.27
  557.6 21.8 reduce-scatter.29
  582.1 21.8 reduce-scatter.35
  606.8 21.8 reduce-scatter.37
  631.4 21.8 reduce-scatter.31
  655.9 21.8 reduce-scatter.33
  680.5 21.8 reduce-scatter.21
  705.0 60.0 reduce-scatter.23
  767.9 60.0 reduce-scatter.25
  834.0 176.9 all-reduce.16
where the time goes:
time: 1050 us; the launch traced here: 1030 us
  waiting for transfers between devices  359 us (34%)
  matrix products  330 us (31%)
  local copies, waits for them, and re-layouts  138 us (13%)
  blocking collectives  109 us (10%)
  other arithmetic  69.8 us (7%)
  between operations  16.5 us (2%)
  loops' own time  10.9 us (1%)
    dot_general x9, matrix products, dot_plain(): return jnp.dot(left, right, preferred_element_type=jnp.float32)  83.5 us
    psum x1, waiting for transfers between devices, local(): lax.psum(shares[0].astype(jnp.bfloat16), 'dp').astype(jnp.float32)  83 us
    unnamed x25, waiting for transfers between devices  80.7 us
    reduce_scatter x1, waiting for transfers between devices, local(): lax.psum_scatter(grad_inner_weight.astype(jnp.bfloat16), 'fsdp', scatter_...  62.8 us
    reduce_scatter x1, waiting for transfers between devices, local(): lax.psum_scatter(grad_down_weight.astype(jnp.bfloat16), 'fsdp', scatter_d...  62.8 us
    psum x1, blocking collectives, local(): lax.psum(shares[4].astype(jnp.bfloat16), 'dp').astype(jnp.float32)  60 us
    unnamed x200, local copies, waits for them, and re-layouts  57.7 us
    dot_general x9, matrix products, dot_back(): lax.dot_general(left, right, (((1,), (1,)), ((), ())), preferred_element_...  52.4 us
  transfers between devices with their start and end apart: 19, of which 12 were waited for; matrix products, arithmetic and copies ran while one was open for 28% of the time, Pallas kernels for 0%

commit v1 on v0

v1 whole, which is shorter than its diff:
```python
import functools
import jax
import jax.numpy as jnp
from jax import lax
from jax.experimental import pallas as pl
from jax.experimental.pallas import tpu as pltpu
from jax.sharding import PartitionSpec as P

HD = 64
WORDS = 512
norm_eps = 1e-12
F32 = jnp.float32
BF16 = jnp.bfloat16
MASKED = -1000000000.0


def nn(a, b):
    return lax.dot_general(a, b, (((1,), (0,)), ((), ())), preferred_element_type=F32)


def nt(a, b):
    return lax.dot_general(a, b, (((1,), (1,)), ((), ())), preferred_element_type=F32)


def vmem(mb):
    return pltpu.CompilerParams(vmem_limit_bytes=mb * 1024 * 1024)


def spans(total, size):
    return [(s, min(size, total - s)) for s in range(0, total, size)]


def project_kernel(x, w, b, qw, qe, k, v):
    words = x[0, :WORDS]
    ents = x[0, WORDS:]
    scale = HD ** -0.5

    def query(rows, i):
        return ((nn(rows, w[i]) + b[i:i + 1]).astype(BF16) * scale).astype(BF16)

    qw[0, :WORDS] = query(words, 0)
    qe[0, :WORDS] = query(words, 1)
    qw[0, WORDS:] = query(ents, 2)
    qe[0, WORDS:] = query(ents, 3)
    k[0] = nn(x[0], w[4]).astype(BF16)
    v[0] = (nn(x[0], w[5]) + b[5:6]).astype(BF16)


def project(x, w, b):
    seqs, length, width = x.shape
    cols = 256
    out = jax.ShapeDtypeStruct((seqs, length, width), BF16)
    spec = pl.BlockSpec((1, length, cols), lambda j, s: (s, 0, j))
    return pl.pallas_call(
        project_kernel,
        grid=(width // cols, seqs),
        in_specs=[
            pl.BlockSpec((1, length, width), lambda j, s: (s, 0, 0)),
            pl.BlockSpec((6, width, cols), lambda j, s: (0, 0, j)),
            pl.BlockSpec((16, cols), lambda j, s: (0, j)),
        ],
        out_specs=[spec] * 4,
        out_shape=[out] * 4,
        compiler_params=vmem(48),
        name="project",
    )(x, w, b)


def head_mask(h):
    lane = lax.broadcasted_iota(jnp.int32, (1, 2 * HD), 1)
    return jnp.where(lane // HD == h, 1.0, 0.0).astype(BF16)


def attend_kernel(segr, segc, qw, qe, k, v, o, lse, bias, *, step):
    @pl.when(pl.program_id(1) == 0)
    def _():
        bias[...] = jnp.where(segc[0] == segr[0], 0.0, MASKED)

    length = k.shape[1]
    kp = k[0]
    vt = v[0].T
    for s, n in spans(length, step):
        parts = []
        for h in range(2):
            kh = kp * head_mask(h)
            st = jnp.concatenate(
                [nt(kh[:WORDS], qw[0, s:s + n]), nt(kh[WORDS:], qe[0, s:s + n])], axis=0
            ) + bias[:, s:s + n]
            peak = jnp.max(st, axis=0, keepdims=True)
            pt = jnp.exp(st - peak)
            total = jnp.sum(pt, axis=0, keepdims=True)
            ot = nn(vt[h * HD:(h + 1) * HD], pt.astype(BF16))
            parts.append(ot * (1.0 / total))
            lse[0, 0, h:h + 1, s:s + n] = peak + jnp.log(total)
        o[0, s:s + n] = jnp.concatenate(parts, axis=0).T.astype(BF16)


def attend(qw, qe, k, v, seg, step=256):
    seqs, length, width = k.shape
    pairs = width // (2 * HD)
    spec = pl.BlockSpec((1, length, 2 * HD), lambda s, h: (s, 0, h))
    return pl.pallas_call(
        functools.partial(attend_kernel, step=step),
        grid=(seqs, pairs),
        in_specs=[
            pl.BlockSpec((1, 1, length), lambda s, h: (s, 0, 0)),
            pl.BlockSpec((1, length, 1), lambda s, h: (s, 0, 0)),
            spec, spec, spec, spec,
        ],
        out_specs=[spec, pl.BlockSpec((1, 1, 2, length), lambda s, h: (s, h, 0, 0))],
        out_shape=[
            jax.ShapeDtypeStruct((seqs, length, width), BF16),
            jax.ShapeDtypeStruct((seqs, pairs, 2, length), F32),
        ],
        scratch_shapes=[pltpu.VMEM((length, length), F32)],
        compiler_params=vmem(48),
        name="attend",
    )(seg[:, None, :], seg[:, :, None], qw, qe, k, v)


def attend_back_kernel(segr, segc, qw, qe, k, v, o, g, lse, dqw, dqe, dk, dv, bias, *, step):
    @pl.when(pl.program_id(1) == 0)
    def _():
        bias[...] = jnp.where(segc[0] == segr[0], 0.0, MASKED)

    length = k.shape[1]
    kp = k[0]
    kt = kp.T
    vp = v[0]
    scale = HD ** -0.5
    dv_sum = None
    for i, (s, n) in enumerate(spans(length, step)):
        qws = qw[0, s:s + n]
        qes = qe[0, s:s + n]
        gs = g[0, s:s + n]
        prod = (gs.astype(F32) * o[0, s:s + n].astype(F32)).T
        dqw_parts = []
        dqe_parts = []
        for h in range(2):
            m = head_mask(h)
            kh = kp * m
            delta = jnp.sum(prod[h * HD:(h + 1) * HD], axis=0, keepdims=True)
            st = jnp.concatenate([nt(kh[:WORDS], qws), nt(kh[WORDS:], qes)], axis=0)
            pt = jnp.exp(st + bias[:, s:s + n] - lse[0, 0, h:h + 1, s:s + n])
            dpt = nt(vp * m, gs)
            dst = (pt * (dpt - delta)).astype(BF16)
            gv = nn(pt.astype(BF16), gs * m)
            gk_w = nn(dst[:WORDS], qws * m)
            gk_e = nn(dst[WORDS:], qes * m)
            kth = kt[h * HD:(h + 1) * HD]
            dqw_parts.append(nn(kth[:, :WORDS], dst[:WORDS]))
            dqe_parts.append(nn(kth[:, WORDS:], dst[WORDS:]))
            if h == 0:
                gv_p, gkw_p, gke_p = gv, gk_w, gk_e
            else:
                gv_p, gkw_p, gke_p = gv_p + gv, gkw_p + gk_w, gke_p + gk_e
        dqw[0, s:s + n] = (jnp.concatenate(dqw_parts, axis=0).T * scale).astype(BF16)
        dqe[0, s:s + n] = (jnp.concatenate(dqe_parts, axis=0).T * scale).astype(BF16)
        if i == 0:
            dv_sum, dkw_sum, dke_sum = gv_p, gkw_p, gke_p
        else:
            dv_sum, dkw_sum, dke_sum = dv_sum + gv_p, dkw_sum + gkw_p, dke_sum + gke_p
    dv[0] = dv_sum.astype(BF16)
    dk[0, :WORDS] = dkw_sum.astype(BF16)
    dk[0, WORDS:] = dke_sum.astype(BF16)


def attend_back(qw, qe, k, v, seg, o, g, lse, step=256):
    seqs, length, width = k.shape
    pairs = width // (2 * HD)
    spec = pl.BlockSpec((1, length, 2 * HD), lambda s, h: (s, 0, h))
    out = jax.ShapeDtypeStruct((seqs, length, width), BF16)
    return pl.pallas_call(
        functools.partial(attend_back_kernel, step=step),
        grid=(seqs, pairs),
        in_specs=[
            pl.BlockSpec((1, 1, length), lambda s, h: (s, 0, 0)),
            pl.BlockSpec((1, length, 1), lambda s, h: (s, 0, 0)),
            spec, spec, spec, spec, spec, spec,
            pl.BlockSpec((1, 1, 2, length), lambda s, h: (s, h, 0, 0)),
        ],
        out_specs=[spec] * 4,
        out_shape=[out] * 4,
        scratch_shapes=[pltpu.VMEM((length, length), F32)],
        compiler_params=vmem(48),
        name="attend_back",
    )(seg[:, None, :], seg[:, :, None], qw, qe, k, v, o, g, lse)


def norm_forward(values):
    center = values - jnp.mean(values, axis=-1, keepdims=True)
    scale = lax.rsqrt(jnp.mean(center * center, axis=-1, keepdims=True) + norm_eps)
    return center * scale, scale


def norm_backward(grad, normed, scale):
    first = jnp.mean(grad, axis=-1, keepdims=True)
    second = jnp.mean(grad * normed, axis=-1, keepdims=True)
    return scale * (grad - first - normed * second)


def gelu_pair(u):
    z = jnp.abs(u) * (0.5 ** 0.5)
    t = 1.0 / (1.0 + 0.3275911 * z)
    e = jnp.exp(u * u * -0.5)
    poly = 0.5 * 1.061405429
    poly = poly * t + 0.5 * -1.453152027
    poly = poly * t + 0.5 * 1.421413741
    poly = poly * t + 0.5 * -0.284496736
    poly = poly * t + 0.5 * 0.254829592
    tail = poly * t * e
    cdf = jnp.where(u < 0, tail, 1.0 - tail)
    return cdf, cdf + u * (e * 0.3989422804014327)


def colsum(v):
    return jnp.sum(v, axis=0, keepdims=True)


OUT_BIAS, GAIN_ATTN, SHIFT_ATTN, DOWN_BIAS, GAIN_FFN, SHIFT_FFN = range(6)


def middle_kernel(x, ctx, cot, wo, wi, wd, small, ib, out, gpre, hl, act, gu, gfed, gatt, gctx,
                  sums, ibsum, slope, *, step):
    @pl.when(pl.program_id(0) == 0)
    def _():
        sums[...] = jnp.zeros_like(sums)
        ibsum[...] = jnp.zeros_like(ibsum)

    def row(i):
        return small[i:i + 1]

    ff = wi.shape[1]
    attended = nn(ctx[...], wo[...]) + row(OUT_BIAS)
    normed_attn, scale_attn = norm_forward(x[...].astype(F32) + attended)
    hidden = normed_attn * row(GAIN_ATTN) + row(SHIFT_ATTN)
    low = hidden.astype(BF16)
    hl[...] = low
    fed = jnp.broadcast_to(row(DOWN_BIAS), hidden.shape)
    for s, n in spans(ff, step):
        u = nn(low, wi[:, s:s + n]) + ib[:, s:s + n]
        cdf, grad = gelu_pair(u)
        slope[:, s:s + n] = grad
        a = (u * cdf).astype(BF16)
        act[:, s:s + n] = a
        fed = fed + nn(a, wd[s:s + n])
    normed_ffn, scale_ffn = norm_forward(hidden + fed)
    out[...] = (normed_ffn * row(GAIN_FFN) + row(SHIFT_FFN)).astype(BF16)
    gy = cot[...].astype(F32)
    sums[GAIN_FFN:GAIN_FFN + 1] += colsum(gy * normed_ffn)
    sums[SHIFT_FFN:SHIFT_FFN + 1] += colsum(gy)
    gsum = norm_backward(gy * row(GAIN_FFN), normed_ffn, scale_ffn)
    gf = gsum.astype(BF16)
    gfed[...] = gf
    sums[DOWN_BIAS:DOWN_BIAS + 1] += colsum(gf.astype(F32))
    ghid = gsum
    for s, n in spans(ff, step):
        d = nt(gf, wd[s:s + n]) * slope[:, s:s + n]
        ibsum[:, s:s + n] += colsum(d)
        d = d.astype(BF16)
        gu[:, s:s + n] = d
        ghid = ghid + nt(d, wi[:, s:s + n])
    sums[GAIN_ATTN:GAIN_ATTN + 1] += colsum(ghid * normed_attn)
    sums[SHIFT_ATTN:SHIFT_ATTN + 1] += colsum(ghid)
    gp = norm_backward(ghid * row(GAIN_ATTN), normed_attn, scale_attn)
    gpre[...] = gp
    ga = gp.astype(BF16)
    gatt[...] = ga
    sums[OUT_BIAS:OUT_BIAS + 1] += colsum(ga.astype(F32))
    gctx[...] = nt(ga, wo[...]).astype(BF16)


def middle(x, ctx, cot, wo, wi, wd, small, ib, rows=256, step=512):
    total, width = x.shape
    ff = wi.shape[1]

    def block(n):
        return pl.BlockSpec((rows, n), lambda i: (i, 0))

    def whole(*shape):
        return pl.BlockSpec(shape, lambda i: (0, 0), pipeline_mode=pl.Buffered(1))

    def out(n, dtype):
        return jax.ShapeDtypeStruct((total, n), dtype)

    return pl.pallas_call(
        functools.partial(middle_kernel, step=step),
        grid=(total // rows,),
        in_specs=[
            block(width), block(width), block(width),
            whole(width, width), whole(width, ff), whole(ff, width),
            whole(8, width), whole(1, ff),
        ],
        out_specs=[
            block(width), block(width), block(width), block(ff), block(ff),
            block(width), block(width), block(width),
            pl.BlockSpec((8, width), lambda i: (0, 0)),
            pl.BlockSpec((1, ff), lambda i: (0, 0)),
        ],
        out_shape=[
            out(width, BF16), out(width, F32), out(width, BF16), out(ff, BF16), out(ff, BF16),
            out(width, BF16), out(width, BF16), out(width, BF16),
            jax.ShapeDtypeStruct((8, width), F32),
            jax.ShapeDtypeStruct((1, ff), F32),
        ],
        scratch_shapes=[pltpu.VMEM((rows, ff), F32)],
        compiler_params=vmem(60),
        name="middle",
    )(x, ctx, cot, wo, wi, wd, small, ib)


def ffn_grads_kernel(hl, gu, act_lo, act_hi, gfed, ctx, gatt, dwi, dwd, dwo, hlt):
    @pl.when(pl.program_id(0) == 0)
    def _():
        hlt[...] = hl[...].T
        dwo[0] = nn(ctx[...].T, gatt[...]).astype(BF16)

    half = act_lo.shape[1]
    dwi[0] = nn(hlt[...], gu[...]).astype(BF16)
    dwd[0, :half] = nn(act_lo[...].T, gfed[...]).astype(BF16)
    dwd[0, half:] = nn(act_hi[...].T, gfed[...]).astype(BF16)


def ffn_grads(hl, gu, act, gfed, ctx, gatt):
    total, width = hl.shape
    count = gu.shape[1] // width
    half = width // 2

    def whole():
        return pl.BlockSpec((total, width), lambda j: (0, 0), pipeline_mode=pl.Buffered(1))

    square = pl.BlockSpec((1, width, width), lambda j: (j, 0, 0))
    return pl.pallas_call(
        ffn_grads_kernel,
        grid=(count,),
        in_specs=[
            whole(),
            pl.BlockSpec((total, width), lambda j: (0, j)),
            pl.BlockSpec((total, half), lambda j: (0, j)),
            pl.BlockSpec((total, half), lambda j: (0, count + j)),
            whole(), whole(), whole(),
        ],
        out_specs=[square, square, pl.BlockSpec((1, width, width), lambda j: (0, 0, 0))],
        out_shape=[
            jax.ShapeDtypeStruct((count, width, width), BF16),
            jax.ShapeDtypeStruct((count, width, width), BF16),
            jax.ShapeDtypeStruct((1, width, width), BF16),
        ],
        scratch_shapes=[pltpu.VMEM((width, total), BF16)],
        compiler_params=vmem(60),
        name="ffn_grads",
    )(hl, gu, act, act, gfed, ctx, gatt)


def input_grads_kernel(dqw, dqe, dk, dv, w, gpre, dx):
    dx[0, :WORDS] = (
        gpre[0, :WORDS] + nt(dqw[0, :WORDS], w[0]) + nt(dqe[0, :WORDS], w[1])
        + nt(dk[0, :WORDS], w[4]) + nt(dv[0, :WORDS], w[5])
    )
    dx[0, WORDS:] = (
        gpre[0, WORDS:] + nt(dqw[0, WORDS:], w[2]) + nt(dqe[0, WORDS:], w[3])
        + nt(dk[0, WORDS:], w[4]) + nt(dv[0, WORDS:], w[5])
    )


def input_grads(dqw, dqe, dk, dv, w, gpre):
    seqs, length, width = dqw.shape
    cols = 256
    full = pl.BlockSpec((1, length, width), lambda j, s: (s, 0, 0))
    part = pl.BlockSpec((1, length, cols), lambda j, s: (s, 0, j))
    return pl.pallas_call(
        input_grads_kernel,
        grid=(width // cols, seqs),
        in_specs=[full] * 4 + [pl.BlockSpec((6, cols, width), lambda j, s: (0, j, 0)), part],
        out_specs=part,
        out_shape=jax.ShapeDtypeStruct((seqs, length, width), F32),
        compiler_params=vmem(48),
        name="input_grads",
    )(dqw, dqe, dk, dv, w, gpre)


def qkv_grads_kernel(x, dqw, dqe, dk, dv, dw, sums, xt):
    seqs, length, width = x.shape

    @pl.when(pl.program_id(0) == 0)
    def _():
        for s in range(seqs):
            xt[s] = x[s].T

    def grad(source, lo, hi):
        total = nn(xt[0, :, lo:hi], source[0, lo:hi])
        for s in range(1, seqs):
            total = total + nn(xt[s, :, lo:hi], source[s, lo:hi])
        return total.astype(BF16)

    def bias(source, lo, hi):
        total = colsum(source[0, lo:hi].astype(F32))
        for s in range(1, seqs):
            total = total + colsum(source[s, lo:hi].astype(F32))
        return total

    for i, (source, lo, hi) in enumerate([
        (dqw, 0, WORDS), (dqe, 0, WORDS), (dqw, WORDS, length), (dqe, WORDS, length),
        (dk, 0, length), (dv, 0, length),
    ]):
        dw[i] = grad(source, lo, hi)
        if i != 4:
            sums[i:i + 1] = bias(source, lo, hi)


def qkv_grads(x, dqw, dqe, dk, dv, cols=256):
    seqs, length, width = x.shape
    part = pl.BlockSpec((seqs, length, cols), lambda j: (0, 0, j))
    return pl.pallas_call(
        qkv_grads_kernel,
        grid=(width // cols,),
        in_specs=[pl.BlockSpec((seqs, length, width), lambda j: (0, 0, 0), pipeline_mode=pl.Buffered(1))]
        + [part] * 4,
        out_specs=[
            pl.BlockSpec((6, width, cols), lambda j: (0, 0, j)),
            pl.BlockSpec((8, cols), lambda j: (0, j)),
        ],
        out_shape=[
            jax.ShapeDtypeStruct((6, width, width), BF16),
            jax.ShapeDtypeStruct((8, width), F32),
        ],
        scratch_shapes=[pltpu.VMEM((seqs, width, length), BF16)],
        compiler_params=vmem(60),
        name="qkv_grads",
    )(x, dqw, dqe, dk, dv)

MESH = pl.DeviceIdType.MESH
UNIT = 384


def place():
    d = lax.axis_index("dp")
    f = lax.axis_index("fsdp")
    bits = {"core": d % 2, "y": (d // 2) % 2, "z0": (d // 4) % 2, "z1": (d // 8) % 2, "x": f}
    peers = {"x": {"fsdp": 1 - f}}
    for name, size in (("core", 1), ("y", 2), ("z0", 4), ("z1", 8)):
        peers[name] = {"dp": d + size - 2 * size * bits[name]}
    return bits, peers


def greet(peers, names):
    barrier = pltpu.get_barrier_semaphore()
    for name in names:
        pl.semaphore_signal(barrier, inc=1, device_id=peers[name], device_id_type=MESH)
    pl.semaphore_wait(barrier, len(names))


def gather_kernel(*refs, units):
    n_own = 1 + max(u[0] for u in units)
    own = refs[:n_own]
    small = refs[n_own]
    w6, wo, wi, wd, table = refs[n_own + 1:n_own + 6]
    held, small_held, send, recv, local, small_sem = refs[n_own + 6:]
    bits, peers = place()
    greet(peers, ("x", "y", "z0", "core"))
    f, c = bits["x"], bits["core"]
    piece = UNIT // 8

    def src(u, rows, size):
        i, kind, k = units[u]
        if kind == "wi":
            return own[i].at[pl.ds(rows, size), k * 768:(k + 1) * 768]
        return own[i].at[pl.ds(k * UNIT + rows, size)]

    def dst(u, half, rows, size):
        i, kind, k = units[u]
        if kind == "w6":
            return w6.at[i, pl.ds(half * UNIT + rows, size)]
        if kind == "wo":
            return wo.at[pl.ds(half * UNIT + rows, size)]
        if kind == "wi":
            return wi.at[pl.ds(half * UNIT + rows, size), k * 768:(k + 1) * 768]
        return wd.at[pl.ds(half * 4 * UNIT + k * UNIT + rows, size)]

    def remote(u, stage, a, b, peer):
        return pltpu.make_async_remote_copy(
            src_ref=a, dst_ref=b, send_sem=send.at[u, stage], recv_sem=recv.at[u, stage],
            device_id=peers[peer], device_id_type=MESH,
        )

    def order(u):
        return ("y", "z0") if u % 2 == 0 else ("z0", "y")

    def copy(u, stage):
        first, second = order(u)
        a, b = bits[first], bits[second]
        mine = (c * 4 + b * 2 + a) * piece
        pair = (c * 4 + b * 2) * piece
        away = (c * 4 + (1 - b) * 2) * piece
        if stage == 0:
            return remote(u, 0, src(u, mine, piece), dst(u, f, mine, piece), "x")
        if stage == 1:
            here = dst(u, 1 - f, mine, piece)
            return remote(u, 1, here, here, first)
        if stage == 2:
            here = dst(u, 1 - f, pair, 2 * piece)
            return remote(u, 2, here, here, second)
        here = dst(u, 1 - f, pair if stage == 3 else away, 2 * piece)
        return remote(u, stage, here, here, "core")

    n = len(units)
    for u in range(n):
        copy(u, 0).start()
    small_copy = pltpu.make_async_remote_copy(
        src_ref=small, dst_ref=table.at[f], send_sem=small_sem.at[0], recv_sem=small_sem.at[1],
        device_id=peers["x"], device_id_type=MESH,
    )
    small_copy.start()

    def load(u):
        return pltpu.make_async_copy(src(u, 0, UNIT), held.at[u], local.at[u])

    def store(u):
        return pltpu.make_async_copy(held.at[u], dst(u, f, 0, UNIT), local.at[u])

    for u in range(n):
        load(u).start()
    small_in = pltpu.make_async_copy(small, small_held, small_sem.at[2])
    small_in.start()
    small_in.wait()
    small_out = pltpu.make_async_copy(small_held, table.at[f], small_sem.at[2])
    small_out.start()
    for t in range(n + 2):
        if t < n:
            copy(t, 0).wait_recv()
            copy(t, 1).start()
            load(t).wait()
            store(t).start()
        if 0 <= t - 1 < n:
            copy(t - 1, 1).wait_recv()
            copy(t - 1, 2).start()
            copy(t - 1, 3).start()
        if 0 <= t - 2 < n:
            copy(t - 2, 2).wait_recv()
            copy(t - 2, 4).start()
    for u in range(n):
        copy(u, 3).wait_recv()
        copy(u, 4).wait_recv()
        for stage in range(5):
            copy(u, stage).wait_send()
        store(u).wait()
    small_copy.wait()
    small_out.wait()


def gather(own, small):
    units = [(i, "w6", 0) for i in range(6)] + [(6, "wo", 0)]
    units += [(7, "wi", k) for k in range(4)] + [(8, "wd", k) for k in range(4)]
    n = len(units)
    any_spec = pl.BlockSpec(memory_space=pl.ANY)
    width = own[0].shape[1]
    ff = own[7].shape[1]
    return pl.pallas_call(
        functools.partial(gather_kernel, units=units),
        in_specs=[any_spec] * 10,
        out_specs=[any_spec] * 5,
        out_shape=[
            jax.ShapeDtypeStruct((6, width, width), BF16),
            jax.ShapeDtypeStruct((width, width), BF16),
            jax.ShapeDtypeStruct((width, ff), BF16),
            jax.ShapeDtypeStruct((ff, width), BF16),
            jax.ShapeDtypeStruct((2,) + small.shape, small.dtype),
        ],
        scratch_shapes=[
            pltpu.VMEM((n, UNIT, width), BF16),
            pltpu.VMEM(small.shape, small.dtype),
            pltpu.SemaphoreType.DMA((n, 5)),
            pltpu.SemaphoreType.DMA((n, 5)),
            pltpu.SemaphoreType.DMA((n,)),
            pltpu.SemaphoreType.DMA((3,)),
        ],
        compiler_params=pltpu.CompilerParams(
            collective_id=0, has_side_effects=True, vmem_limit_bytes=48 * 1024 * 1024
        ),
        name="gather_params",
    )(*own, small)


STAGES = ("core", "x", "y", "z0", "z1")
BACK = ("z1", "z0", "y", "core")


def reduce_kernel(*refs, counts, has_small):
    n_in = len(counts)
    grads = refs[:n_in]
    if has_small:
        small_in, out, small_out = refs[n_in:n_in + 3]
        rest = refs[n_in + 3:]
    else:
        out = refs[n_in]
        rest = refs[n_in + 1:]
    own, from_core, from_x, from_y, from_z0, from_z1, full, send, recv, local = rest[:10]
    if has_small:
        small_sum, small_got, small_send, small_recv = rest[10:]
    bits, peers = place()
    greet(peers, STAGES)
    half = UNIT
    c, f = bits["core"], bits["x"]
    total = sum(counts)
    mine = pl.multiple_of(c * half, half)
    theirs = pl.multiple_of((1 - c) * half, half)

    def remote(u, stage, a, b, peer):
        return pltpu.make_async_remote_copy(
            src_ref=a, dst_ref=b, send_sem=send.at[u, stage], recv_sem=recv.at[u, stage],
            device_id=peers[peer], device_id_type=MESH,
        )

    y0 = bits["y"] * 192
    z00 = y0 + bits["z0"] * 96
    z10 = z00 + bits["z1"] * 48
    y1 = (1 - bits["y"]) * 192
    z01 = y0 + (1 - bits["z0"]) * 96
    z11 = z00 + (1 - bits["z1"]) * 48

    def rows(start, size):
        return pl.ds(pl.multiple_of(start, 16), size)

    def first(g, k, u):
        return remote(u, 0, g.at[k, :, pl.ds(theirs, half)], from_core.at[u], "core")

    def load(g, k, u):
        return pltpu.make_async_copy(g.at[k, :, pl.ds(mine, half)], own.at[u], local.at[u])

    def copy(u, stage):
        if stage == 1:
            return remote(u, 1, own.at[u, rows((1 - f) * UNIT, UNIT)], from_x.at[u], "x")
        if stage == 2:
            return remote(u, 2, own.at[u, rows(f * UNIT + y1, 192)], from_y.at[u], "y")
        if stage == 3:
            return remote(u, 3, own.at[u, rows(f * UNIT + z01, 96)], from_z0.at[u], "z0")
        if stage == 4:
            return remote(u, 4, own.at[u, rows(f * UNIT + z11, 48)], from_z1.at[u], "z1")
        start, size, peer = {5: (z10, 48, "z1"), 6: (z00, 96, "z0"), 7: (y0, 192, "y"), 8: (0, 384, "core")}[stage]
        here = full.at[u, rows(start, size), pl.ds(mine, half)]
        return remote(u, stage, here, here, peer)

    def add(u, start, size, got):
        here = rows(start, size)
        own[u, here] = (own[u, here].astype(F32) + got.astype(F32)).astype(BF16)

    base = 0
    for g, count in zip(grads, counts):
        def begin(k, carry, g=g, base=base):
            first(g, k, base + k).start()
            load(g, k, base + k).start()
            return carry
        lax.fori_loop(0, count, begin, 0)
        base += count

    def small_copy(s):
        return pltpu.make_async_remote_copy(
            src_ref=small_sum.at[s], dst_ref=small_got.at[s], send_sem=small_send.at[s],
            recv_sem=small_recv.at[s], device_id=peers[STAGES[s]], device_id_type=MESH,
        )

    if has_small:
        small_sum[0] = small_in[...]
        small_copy(0).start()

    def out_copy(u):
        return pltpu.make_async_copy(full.at[u], out.at[u], local.at[u])

    def step(t, carry):
        @pl.when(t < total)
        def _():
            u = t
            first(grads[0], 0, u).wait_recv()
            load(grads[0], 0, u).wait()
            for k in range(2):
                add(u, k * UNIT, UNIT, from_core[u, k * UNIT:(k + 1) * UNIT])
            copy(u, 1).start()

        def at(lag, body):
            @pl.when(jnp.logical_and(t >= lag, t < total + lag))
            def _():
                body(t - lag)

        def after_x(u):
            copy(u, 1).wait_recv()
            add(u, f * UNIT, UNIT, from_x[u])
            copy(u, 2).start()

        def after_y(u):
            copy(u, 2).wait_recv()
            add(u, f * UNIT + y0, 192, from_y[u])
            copy(u, 3).start()

        def after_z0(u):
            copy(u, 3).wait_recv()
            add(u, f * UNIT + z00, 96, from_z0[u])
            copy(u, 4).start()

        def after_z1(u):
            copy(u, 4).wait_recv()
            here = rows(f * UNIT + z10, 48)
            full[u, rows(z10, 48), pl.ds(mine, half)] = (
                own[u, here].astype(F32) + from_z1[u].astype(F32)
            ).astype(BF16)
            copy(u, 5).start()

        def forward(stage):
            def body(u):
                copy(u, stage).wait_recv()
                copy(u, stage + 1).start()
            return body

        def finish(u):
            copy(u, 8).wait_recv()
            out_copy(u).start()

        at(2, after_x)
        at(3, after_y)
        at(4, after_z0)
        at(5, after_z1)
        at(6, forward(5))
        at(7, forward(6))
        at(8, forward(7))
        at(9, finish)

        if has_small:
            for s in range(5):
                @pl.when(t == 1 + s)
                def _(s=s):
                    small_copy(s).wait_recv()
                    value = small_sum[s] + small_got[s]
                    if s < 4:
                        small_sum[s + 1] = value
                        small_copy(s + 1).start()
                    else:
                        small_out[...] = value
        return carry

    lax.fori_loop(0, total + 9, step, 0)

    def drain(u, carry):
        first(grads[0], 0, u).wait_send()
        for stage in range(1, 9):
            copy(u, stage).wait_send()
        out_copy(u).wait()
        return carry

    lax.fori_loop(0, total, drain, 0)
    if has_small:
        for s in range(5):
            small_copy(s).wait_send()


def reduce_grads(grads, small=None, collective_id=1):
    counts = [g.shape[0] for g in grads]
    total = sum(counts)
    width = grads[0].shape[2]
    any_spec = pl.BlockSpec(memory_space=pl.ANY)
    vm = pl.BlockSpec(memory_space=pltpu.VMEM)
    has_small = small is not None
    scratch = [
        pltpu.VMEM((total, 2 * UNIT, UNIT), BF16),
        pltpu.VMEM((total, 2 * UNIT, UNIT), BF16),
        pltpu.VMEM((total, 384, UNIT), BF16),
        pltpu.VMEM((total, 192, UNIT), BF16),
        pltpu.VMEM((total, 96, UNIT), BF16),
        pltpu.VMEM((total, 48, UNIT), BF16),
        pltpu.VMEM((total, 384, 2 * UNIT), BF16),
        pltpu.SemaphoreType.DMA((total, 9)),
        pltpu.SemaphoreType.DMA((total, 9)),
        pltpu.SemaphoreType.DMA((total,)),
    ]
    out_shape = [jax.ShapeDtypeStruct((total, UNIT, width), BF16)]
    if has_small:
        scratch += [
            pltpu.VMEM((5,) + small.shape, F32),
            pltpu.VMEM((5,) + small.shape, F32),
            pltpu.SemaphoreType.DMA((5,)),
            pltpu.SemaphoreType.DMA((5,)),
        ]
        out_shape.append(jax.ShapeDtypeStruct(small.shape, F32))
    res = pl.pallas_call(
        functools.partial(reduce_kernel, counts=counts, has_small=has_small),
        in_specs=[any_spec] * len(grads) + [vm] * has_small,
        out_specs=[any_spec] + [vm] * has_small,
        out_shape=out_shape,
        scratch_shapes=scratch,
        compiler_params=pltpu.CompilerParams(
            collective_id=collective_id, has_side_effects=True, vmem_limit_bytes=60 * 1024 * 1024
        ),
        name="reduce_grads",
    )(*grads, *([small] if has_small else []))
    return res if has_small else res[0]


def local(
    inputs, segments,
    query_wordword, query_wordent, query_entword, query_entent,
    bias_wordword, bias_wordent, bias_entword, bias_entent,
    key_weight, value_weight, value_bias, out_weight, out_bias,
    gain_attn, shift_attn, inner_weight, inner_bias, down_weight, down_bias,
    gain_ffn, shift_ffn, cotangent, *, dp, fsdp,
):
    seqs, length, width = inputs.shape
    share = width // fsdp
    ff = inner_weight.shape[1]
    paired = dp == 16 and fsdp == 2

    def gather_all(value):
        return lax.all_gather(value, "fsdp", axis=0, tiled=True)

    zero = jnp.zeros((share,), BF16)
    packed = jnp.concatenate([
        jnp.stack([
            bias_wordword, bias_wordent, bias_entword, bias_entent, zero, value_bias,
            out_bias, gain_attn, shift_attn, down_bias, gain_ffn, shift_ffn,
        ]),
        inner_bias.reshape(4, share),
    ])
    own = (query_wordword, query_wordent, query_entword, query_entent, key_weight, value_weight,
           out_weight, inner_weight, down_weight)
    if paired:
        w6, wo, wi, wd, table = gather(own, packed)
    else:
        w6 = jnp.stack([gather_all(w) for w in own[:6]])
        wo, wi, wd = [gather_all(w) for w in own[6:]]
        table = lax.all_gather(packed, "fsdp", axis=0)
    wide = table.transpose(1, 0, 2).reshape(16, width).astype(F32)
    ib = table[:, 12:].reshape(1, ff).astype(F32)

    qw, qe, keys, vals = project(inputs, w6, wide)
    ctx, lse = attend(qw, qe, keys, vals, segments)

    def flat(value):
        return value.reshape(seqs * length, width)

    ctx_rows = flat(ctx)
    out, gpre, hl, act, gu, gfed, gatt, gctx, sums, ibsum = middle(
        flat(inputs), ctx_rows, flat(cotangent), wo, wi, wd, wide[6:14], ib)
    units = ffn_grads(hl, gu, act, gfed, ctx_rows, gatt)
    dqw, dqe, dk, dv = attend_back(
        qw, qe, keys, vals, segments, ctx, gctx.reshape(inputs.shape), lse)
    grad_inputs = input_grads(dqw, dqe, dk, dv, w6, gpre.reshape(inputs.shape))
    dw6, qsums = qkv_grads(inputs, dqw, dqe, dk, dv)
    small = jnp.concatenate([sums, qsums, ibsum.reshape(4, width), jnp.zeros((4, width), F32)])
    f = lax.axis_index("fsdp")

    if paired:
        grads, totals = reduce_grads([*units, dw6], small)
        grads = grads.astype(F32)
        g_wi = grads[:4].transpose(1, 0, 2).reshape(share, ff)
        g_wd = grads[4:8].reshape(4 * share, width)
        g_wo = grads[8]
        g6 = [grads[9 + i] for i in range(6)]
    else:
        def shared(grad):
            part = lax.psum_scatter(grad, "fsdp", scatter_dimension=0, tiled=True)
            return lax.psum(part, "dp").astype(F32)

        g_wi = shared(units[0].transpose(1, 0, 2).reshape(width, ff))
        g_wd = shared(units[1].reshape(4, 2, width // 2, width).transpose(1, 0, 2, 3).reshape(ff, width))
        g_wo = shared(units[2][0])
        g6 = [shared(dw6[i]) for i in range(6)]
        totals = lax.psum(small, ("dp", "fsdp"))

    mine = lax.dynamic_slice_in_dim(totals[:16], f * share, share, axis=1)
    g_ib = lax.dynamic_slice_in_dim(totals[16:20].reshape(ff), f * (ff // fsdp), ff // fsdp)
    return (
        out.reshape(inputs.shape), grad_inputs,
        g6[0], g6[1], g6[2], g6[3],
        mine[8], mine[9], mine[10], mine[11],
        g6[4], g6[5], mine[13],
        g_wo, mine[OUT_BIAS], mine[GAIN_ATTN], mine[SHIFT_ATTN],
        g_wi, g_ib, g_wd, mine[DOWN_BIAS], mine[GAIN_FFN], mine[SHIFT_FFN],
    )


def solution(mesh):
    rows = P(("dp", "fsdp"), None, None)
    mat = P("fsdp", None)
    vec = P("fsdp")
    params = (mat,) * 4 + (vec,) * 4 + (mat, mat, vec, mat, vec, vec, vec, mat, vec, mat, vec, vec, vec)
    return jax.shard_map(
        functools.partial(local, dp=mesh.shape["dp"], fsdp=mesh.shape["fsdp"]),
        mesh=mesh,
        in_specs=(rows, P(("dp", "fsdp"), None)) + params + (rows,),
        out_specs=(rows, rows) + params,
        check_vma=False,
    )
```

time: 1050 us -> 462 us (0.44); the launches traced: 1030 us -> 461 us
  Pallas kernels: 0 us -> 390 us
  waiting for transfers between devices: 359 us -> 0 us
  matrix products: 330 us -> 0 us
  blocking collectives: 109 us -> 0 us
  local copies, waits for them, and re-layouts: 138 us -> 56.5 us
  other arithmetic: 69.8 us -> 13.6 us
  between operations: 16.5 us -> 0.83 us
  loops' own time: 10.9 us -> 0 us
    pallas_call x0 -> x9, Pallas kernels: none -> 390 us  [the longest x1 137 us: reduce_grads(): pl.pallas_call(functools.partial(reduce_kernel, counts=counts, has_small=...]
    dot_general x63 -> x0, matrix products: 278 us -> none  [the longest x9 83.5 us: dot_plain(): return jnp.dot(left, right, preferred_element_type=jnp.float32)]
    reduce_scatter x3 -> x0, waiting for transfers between devices: 148 us -> none  [the longest x1 62.8 us: local(): lax.psum_scatter(grad_inner_weight.astype(jnp.bfloat16), 'fsdp', scatter_...]
    psum x1 -> x0, waiting for transfers between devices: 83 us -> none  [local(): lax.psum(shares[0].astype(jnp.bfloat16), 'dp').astype(jnp.float32)]
    unnamed x25 -> x0, waiting for transfers between devices: 80.7 us -> none
    psum x1 -> x0, blocking collectives: 60 us -> none  [local(): lax.psum(shares[4].astype(jnp.bfloat16), 'dp').astype(jnp.float32)]
    sub x2 -> x0, matrix products: 51.7 us -> none  [attend_back(): grad_scores = (prob * (grad_prob - delta)).astype(jnp.bfloat16)]
    all_gather x9 -> x0, waiting for transfers between devices: 46.9 us -> none  [the longest x1 21.9 us: local(): lax.all_gather(query_entent, 'fsdp', axis=0, tiled=True)]
  transfers between devices with their start and end apart: 19 -> 0, of which waited for: 12 -> 0; matrix products, arithmetic and copies ran while one was open for 28% -> 0% of each run, Pallas kernels for 0% -> 0%
where the time goes in v1:
time: 462 us; the launch traced here: 461 us
  Pallas kernels  390 us (84%)
  local copies, waits for them, and re-layouts  56.5 us (12%)
  other arithmetic  13.6 us (3%)
    pallas_call x1, Pallas kernels, reduce_grads(): pl.pallas_call(functools.partial(reduce_kernel, counts=counts, has_small=...  137 us
    pallas_call x1, Pallas kernels, gather(): pl.pallas_call(functools.partial(gather_kernel, units=units), in_specs=[a...  64.6 us
    pallas_call x1, Pallas kernels, middle(): pl.pallas_call(functools.partial(middle_kernel, step=step), grid=(total /...  58.8 us
    pallas_call x1, Pallas kernels, attend_back(): pl.pallas_call(functools.partial(attend_back_kernel, step=step), grid=(se...  36.9 us
    pallas_call x1, Pallas kernels, attend(): pl.pallas_call(functools.partial(attend_kernel, step=step), grid=(seqs, p...  33 us
    unnamed x41, local copies, waits for them, and re-layouts  21.4 us
    pallas_call x1, Pallas kernels, ffn_grads(): pl.pallas_call(ffn_grads_kernel, grid=(count,), in_specs=[whole(), pl.Blo...  20.6 us
    pallas_call x1, Pallas kernels, input_grads(): pl.pallas_call(input_grads_kernel, grid=(width // cols, seqs), in_specs=[...  13.4 us

profile of v1, /device:TPU:1, one launch (start us, length us, event | category | flops | bytes accessed | tf_op | source)
XLA Modules:
  0.0 460.9 jit_solution(3718646753913982087)
XLA Ops:
  0.7 0.7 broadcast_in_dim.11.segr
  1.4 0.9 copy.49.segc
  2.3 0.7 stack.33
  3.0 0.7 stack.34
  3.7 0.7 stack.35
  4.4 0.7 stack.36
  5.1 0.7 stack.37
  5.7 0.7 stack.38
  6.4 0.7 stack.39
  7.1 0.7 stack.40
  7.8 0.7 stack.41
  8.5 0.7 stack.42
  9.2 0.7 stack.43
  9.8 0.7 reshape.98
  10.6 1.1 copy-done.10
  11.7 1.1 copy-done.11
  12.8 1.1 copy-done.12
  13.8 1.1 copy-done.13
  14.9 1.1 copy-done.14
  15.9 1.1 copy-done.15
  17.0 1.1 copy-done.16
  18.1 64.6 %gather_params.1 = (bf16[6,768,768]{2,1,0:T(8,128)(2,1)}, bf16[768,768]{1,0:T(8,128)(2,1)S(1)}, bf16[768,3072]{1,0:T(8,128)(2,1)}, bf16[3072,768]{1,0:T(8,128)(2,1)}, bf16[2,16,384]{2,1,0:T(8,128)(2,1)S(1)}) custom-call(bf16[384,768]{1,0:T(8,128)(2,1)S(1)} %copy-done.10, bf16[384,768]{1,0:T(8,128)(2,1)S(1)} %copy-done.11, bf16[384,768]{1,0:T(8,128)(2,1)S(1)} %copy-done.12, ...), custom_call_target="tpu_custom_call" | custom-call | tf_op jit(solution)/shard_map/gather_params/pallas_call | solution.py:558
  82.8 12.3 %project.1 = (bf16[2,640,768]{2,1,0:T(8,128)(2,1)S(1)}, bf16[2,640,768]{2,1,0:T(8,128)(2,1)S(1)}, bf16[2,640,768]{2,1,0:T(8,128)(2,1)S(1)}, bf16[2,640,768]{2,1,0:T(8,128)(2,1)}) custom-call(bf16[2,640,768]{2,1,0:T(8,128)(2,1)} %x.3, bf16[6,768,768]{2,1,0:T(8,128)(2,1)} %get-tuple-element.55.w, f32[16,768]{1,0:T(8,128)S(1)} %bitcast.33), custom_call_target="tpu_custom_call" | custom-call | tf_op jit(solution)/shard_map/project/pallas_call | solution.py:54
  95.1 1.3 copy-done.2
  96.4 1.3 copy-done.3
  97.7 33.0 %attend.1 = (bf16[2,640,768]{2,1,0:T(8,128)(2,1)S(1)}, f32[2,6,2,640]{3,2,1,0:T(2,128)S(1)}) custom-call(s32[2,1,640]{2,1,0:T(1,128)S(1)} %broadcast_in_dim.11.segr, s32[2,640,1]{2,1,0:T(8,128)S(1)} %copy.49.segc, bf16[2,640,768]{2,1,0:T(8,128)(2,1)S(1)} %get-tuple-element.57.qw, bf16[2,640,768]{2,1,0:T(8,128)(2,1)} %copy-done.2, ...), custom_call_target="tpu_custom_call" | custom-call | tf_op jit(solution)/shard_map/attend/pallas_call | solution.py:102
  130.7 1.3 copy-done
  132.0 0.6 slice.100
  132.6 0.6 reshape.108.ib
  133.2 58.8 %middle.1 = (bf16[1280,768]{1,0:T(8,128)(2,1)}, f32[1280,768]{1,0:T(8,128)}, bf16[1280,768]{1,0:T(8,128)(2,1)}, bf16[1280,3072]{1,0:T(8,128)(2,1)}, bf16[1280,30...) custom-call(bf16[1280,768]{1,0:T(8,128)(2,1)} %bitcast.35, ...), custom_call_target="tpu_custom_call" | custom-call | tf_op jit(solution)/shard_map/middle/pallas_call | solution.py:286
  192.1 1.1 copy-done.8
  193.2 36.9 %attend_back.1 = (bf16[2,640,768]{2,1,0:T(8,128)(2,1)S(1)}, bf16[2,640,768]{2,1,0:T(8,128)(2,1)S(1)}, bf16[2,640,768]{2,1,0:T(8,128)(2,1)}, bf16[2,640,768]{2,1,0:T(8,128)(2,1)}) custom-call(s32[2,1,640]{2,1,0:T(1,128)S(1)} %broadcast_in_dim.11.segr, s32[2,640,1]{2,1,0:T(8,128)S(1)} %copy-done.8, bf16[2,640,768]{2,1,0:T(8,128)(2,1)} %copy-done.1, ...), custom_call_target="tpu_custom_call" | custom-call | tf_op jit(solution)/shard_map/attend_back/pallas_call | solution.py:173
  230.1 3.0 copy-done.6
  233.0 13.4 %input_grads.1 = f32[2,640,768]{2,1,0:T(8,128)} custom-call(bf16[2,640,768]{2,1,0:T(8,128)(2,1)S(1)} %get-tuple-element.68.dqw, bf16[2,640,768]{2,1,0:T(8,128)(2,1)S(1)} %get-tuple-element.69.dqe, bf16[2,640,768]{2,1,0:T(8,128)(2,1)S(1)} %copy-done.6, bf16[2,640,768]{2,1,0:T(8,128)(2,1)} %get-tuple-element.71.dv, bf16[6,768,768]{2,1,0:T(8,128)(2,1)} %get-tuple-element.55.w, ...), custom_call_target="tpu_custom_call" | custom-call | tf_op jit(solution)/shard_map/input_grads/pallas_call | solution.py:371
  246.5 20.6 %ffn_grads.1 = (bf16[4,768,768]{2,1,0:T(8,128)(2,1)}, bf16[4,768,768]{2,1,0:T(8,128)(2,1)}, bf16[1,768,768]{2,1,0:T(8,128)(2,1)}) custom-call(bf16[1280,768]{1,0:T(8,128)(2,1)} %get-tuple-element.73.hl, bf16[1280,3072]{1,0:T(8,128)(2,1)} %get-tuple-element.74.gu, bf16[1280,3072]{1,0:T(8,128)(2,1)} %get-tuple-element.75.act_lo.act_hi, ...), custom_call_target="tpu_custom_call" | custom-call | tf_op jit(solution)/shard_map/ffn_grads/pallas_call | solution.py:333
  267.1 13.2 %qkv_grads.1 = (bf16[6,768,768]{2,1,0:T(8,128)(2,1)}, f32[8,768]{1,0:T(8,128)}) custom-call(bf16[2,640,768]{2,1,0:T(8,128)(2,1)} %x.3, bf16[2,640,768]{2,1,0:T(8,128)(2,1)} %copy-done.4, bf16[2,640,768]{2,1,0:T(8,128)(2,1)} %copy-done.5, bf16[2,640,768]{2,1,0:T(8,128)(2,1)} %get-tuple-element.70.dk, bf16[2,640,768]{2,1,0:T(8,128)(2,1)} %get-tuple-element.71.dv), custom_call_target="tpu_custom_call" | custom-call | tf_op jit(solution)/shard_map/qkv_grads/pallas_call | solution.py:414
  280.2 0.5 broadcast.16
  280.7 0.7 reduce.25
  281.5 1.4 maximum_maximum_fusion.refs_4_
  283.0 137.1 %reduce_grads.1 = (bf16[15,384,768]{2,1,0:T(8,128)(2,1)}, f32[24,768]{1,0:T(8,128)}) custom-call(bf16[4,768,768]{2,1,0:T(8,128)(2,1)} %get-tuple-element.78.refs_0_, bf16[4,768,768]{2,1,0:T(8,128)(2,1)} %get-tuple-element.79.refs_1_, bf16[1,768,768]{2,1,0:T(8,128)(2,1)} %get-tuple-element.80.refs_2_, bf16[6,768,768]{2,1,0:T(8,128)(2,1)} %get-tuple-element.81.refs_3_, ...), custom_call_target="tpu_custom_call" | custom-call | tf_op jit(solution)/shard_map/reduce_grads/pallas_call | solution.py:782
  420.1 11.5 %convert_element_type.20 = f32[15,384,768]{2,1,0:T(8,128)} convert(bf16[15,384,768]{2,1,0:T(8,128)(2,1)} %get-tuple-element.85) | non-fusion elementwise | flops 4423680 | bytes 26542080 | tf_op jit(solution)/shard_map/convert_element_type | solution.py:850
  431.6 6.8 %slice_bitcast_fusion.1 = (f32[384,768]{1,0:T(8,128)}, f32[384,768]{1,0:T(8,128)}, f32[384,768]{1,0:T(8,128)}, f32[384,768]{1,0:T(8,128)}, f32[384,768]{1,0:T(8,...) fusion(f32[15,384,768]{2,1,0:T(8,128)} %convert_element_type.20), kind=kLoop, calls=%fused_computation.1 | loop fusion | bytes 16515072 | tf_op jit(solution)/shard_map/squeeze | solution.py:853
  438.3 0.7 dynamic-slice_reduce_fusion
  439.0 4.8 %slice_bitcast_fusion = f32[384,4,768]{2,0,1:T(8,128)} fusion(f32[15,384,768]{2,1,0:T(8,128)} %convert_element_type.20), kind=kLoop, calls=%fused_computation | loop fusion | bytes 9437184 | tf_op jit(solution)/shard_map/transpose | solution.py:851
  443.9 6.1 %copy.51 = f32[384,4,768]{0,2,1:T(8,128)} copy(f32[384,4,768]{2,0,1:T(8,128)} %slice_bitcast_fusion) | data formatting | bytes 9437184 | tf_op jit(solution)/shard_map/transpose | solution.py:851
  449.9 6.0 %copy.52 = f32[384,3072]{1,0:T(8,128)} copy(f32[384,3072]{0,1:T(8,128)} %bitcast.34) | data formatting | bytes 9437184
  456.0 0.7 dynamic_slice.7
  456.7 4.3 slice.109
  (39 shorter events, 0.3 us)
Async XLA Ops:
  2.3 95.4 %copy-start.7 = (s32[2,640,1]{2,1,0:T(8,128)}, s32[2,640,1]{2,1,0:T(8,128)S(1)}, u32[]{:S(2)}) copy-start(s32[2,640,1]{2,1,0:T(8,128)S(1)} %copy.49.segc) | copy-start | bytes 15364
  10.6 1.1 copy-start.10
  11.7 1.1 copy-start.11
  12.7 1.1 copy-start.12
  13.8 1.1 copy-start.13
  14.9 1.1 copy-start.14
  15.9 1.1 copy-start.15
  17.0 1.1 copy-start.16
  82.7 12.4 %copy-start.9 = (bf16[768,768]{1,0:T(8,128)(2,1)}, bf16[768,768]{1,0:T(8,128)(2,1)S(1)}, u32[]{:S(2)}) copy-start(bf16[768,768]{1,0:T(8,128)(2,1)S(1)} %get-tuple-element.62.wo) | copy-start | bytes 3538948
  95.1 1.3 copy-start.2
  96.4 1.3 copy-start.3
  97.7 33.1 %copy-start.1 = (bf16[2,640,768]{2,1,0:T(8,128)(2,1)}, bf16[2,640,768]{2,1,0:T(8,128)(2,1)S(1)}, u32[]{:S(2)}) copy-start(bf16[2,640,768]{2,1,0:T(8,128)(2,1)S(1)} %get-tuple-element.57.qw) | copy-start | bytes 5898244
  130.7 1.3 copy-start
  192.1 1.1 copy-start.8
  230.1 16.4 %copy-start.4 = (bf16[2,640,768]{2,1,0:T(8,128)(2,1)}, bf16[2,640,768]{2,1,0:T(8,128)(2,1)S(1)}, u32[]{:S(2)}) copy-start(bf16[2,640,768]{2,1,0:T(8,128)(2,1)S(1)} %get-tuple-element.68.dqw) | copy-start | bytes 5898244
  230.1 16.4 %copy-start.5 = (bf16[2,640,768]{2,1,0:T(8,128)(2,1)}, bf16[2,640,768]{2,1,0:T(8,128)(2,1)S(1)}, u32[]{:S(2)}) copy-start(bf16[2,640,768]{2,1,0:T(8,128)(2,1)S(1)} %get-tuple-element.69.dqe) | copy-start | bytes 5898244
  230.1 3.0 copy-start.6
  267.1 13.7 %copy-start.19 = (f32[1,3072]{1,0:T(1,128)S(1)}, f32[1,3072]{1,0:T(1,128)}, u32[]{:S(2)}) copy-start(f32[1,3072]{1,0:T(1,128)} %get-tuple-element.84) | copy-start | bytes 36868
  267.1 14.5 %copy-start.18 = (f32[8,768]{1,0:T(8,128)S(1)}, f32[8,768]{1,0:T(8,128)}, u32[]{:S(2)}) copy-start(f32[8,768]{1,0:T(8,128)} %get-tuple-element.82) | copy-start | bytes 73732
  431.6 6.8 %copy-start.17 = (f32[24,768]{1,0:T(8,128)S(1)}, f32[24,768]{1,0:T(8,128)}, u32[]{:S(2)}) copy-start(f32[24,768]{1,0:T(8,128)} %get-tuple-element.86) | copy-start | bytes 221188

commit v2 on v1

v2 whole, which is shorter than its diff:
```python
import functools
import jax
import jax.numpy as jnp
from jax import lax
from jax.experimental import pallas as pl
from jax.experimental.pallas import tpu as pltpu
from jax.sharding import PartitionSpec as P

HD = 64
WORDS = 512
norm_eps = 1e-12
F32 = jnp.float32
BF16 = jnp.bfloat16
MASKED = -1000000000.0


def nn(a, b):
    return lax.dot_general(a, b, (((1,), (0,)), ((), ())), preferred_element_type=F32)


def nt(a, b):
    return lax.dot_general(a, b, (((1,), (1,)), ((), ())), preferred_element_type=F32)


def vmem(mb):
    return pltpu.CompilerParams(vmem_limit_bytes=mb * 1024 * 1024)


def spans(total, size):
    return [(s, min(size, total - s)) for s in range(0, total, size)]


def project_kernel(x, w, b, qw, qe, k, v):
    words = x[0, :WORDS]
    ents = x[0, WORDS:]
    scale = HD ** -0.5

    def query(rows, i):
        return ((nn(rows, w[i]) + b[i:i + 1]).astype(BF16) * scale).astype(BF16)

    qw[0, :WORDS] = query(words, 0)
    qe[0, :WORDS] = query(words, 1)
    qw[0, WORDS:] = query(ents, 2)
    qe[0, WORDS:] = query(ents, 3)
    k[0] = nn(x[0], w[4]).astype(BF16)
    v[0] = (nn(x[0], w[5]) + b[5:6]).astype(BF16)


def project(x, w, b):
    seqs, length, width = x.shape
    cols = 256
    out = jax.ShapeDtypeStruct((seqs, length, width), BF16)
    spec = pl.BlockSpec((1, length, cols), lambda j, s: (s, 0, j))
    return pl.pallas_call(
        project_kernel,
        grid=(width // cols, seqs),
        in_specs=[
            pl.BlockSpec((1, length, width), lambda j, s: (s, 0, 0)),
            pl.BlockSpec((6, width, cols), lambda j, s: (0, 0, j)),
            pl.BlockSpec((16, cols), lambda j, s: (0, j)),
        ],
        out_specs=[spec] * 4,
        out_shape=[out] * 4,
        compiler_params=vmem(48),
        name="project",
    )(x, w, b)


def head_mask(h):
    lane = lax.broadcasted_iota(jnp.int32, (1, 2 * HD), 1)
    return jnp.where(lane // HD == h, 1.0, 0.0).astype(BF16)


def document_bias(seg):
    row = seg.astype(F32)
    col = jnp.broadcast_to(row, (8, row.shape[1])).T[:, :1]
    return jnp.where(col == row, 0.0, MASKED)


def attend_kernel(seg, qw, qe, k, v, o, lse, bias, *, step):
    @pl.when(pl.program_id(1) == 0)
    def _():
        bias[...] = document_bias(seg[0])

    length = k.shape[1]
    kp = k[0]
    vt = v[0].T
    for s, n in spans(length, step):
        parts = []
        for h in range(2):
            kh = kp * head_mask(h)
            st = jnp.concatenate(
                [nt(kh[:WORDS], qw[0, s:s + n]), nt(kh[WORDS:], qe[0, s:s + n])], axis=0
            ) + bias[:, s:s + n]
            peak = jnp.max(st, axis=0, keepdims=True)
            pt = jnp.exp(st - peak)
            total = jnp.sum(pt, axis=0, keepdims=True)
            ot = nn(vt[h * HD:(h + 1) * HD], pt.astype(BF16))
            parts.append(ot * (1.0 / total))
            lse[0, 0, h:h + 1, s:s + n] = peak + jnp.log(total)
        o[0, s:s + n] = jnp.concatenate(parts, axis=0).T.astype(BF16)


def attend(qw, qe, k, v, seg, step=256):
    seqs, length, width = k.shape
    pairs = width // (2 * HD)
    spec = pl.BlockSpec((1, length, 2 * HD), lambda s, h: (s, 0, h))
    return pl.pallas_call(
        functools.partial(attend_kernel, step=step),
        grid=(seqs, pairs),
        in_specs=[
            pl.BlockSpec((1, 1, length), lambda s, h: (s, 0, 0)),
            spec, spec, spec, spec,
        ],
        out_specs=[spec, pl.BlockSpec((1, 1, 2, length), lambda s, h: (s, h, 0, 0))],
        out_shape=[
            jax.ShapeDtypeStruct((seqs, length, width), BF16),
            jax.ShapeDtypeStruct((seqs, pairs, 2, length), F32),
        ],
        scratch_shapes=[pltpu.VMEM((length, length), F32)],
        compiler_params=vmem(48),
        name="attend",
    )(seg[:, None, :], qw, qe, k, v)


def attend_back_pair(qw, qe, k, v, o, g, lse, bias, put, step):
    length = k.shape[1]
    kp = k[0]
    kt = kp.T
    vp = v[0]
    scale = HD ** -0.5
    sums = None
    for s, n in spans(length, step):
        qws = qw[0, s:s + n]
        qes = qe[0, s:s + n]
        gs = g[0, s:s + n]
        prod = (gs.astype(F32) * o[0, s:s + n].astype(F32)).T
        dqw_parts = []
        dqe_parts = []
        for h in range(2):
            m = head_mask(h)
            kh = kp * m
            delta = jnp.sum(prod[h * HD:(h + 1) * HD], axis=0, keepdims=True)
            st = jnp.concatenate([nt(kh[:WORDS], qws), nt(kh[WORDS:], qes)], axis=0)
            pt = jnp.exp(st + bias[:, s:s + n] - lse[0, 0, h:h + 1, s:s + n])
            dpt = nt(vp * m, gs)
            dst = (pt * (dpt - delta)).astype(BF16)
            parts = (nn(pt.astype(BF16), gs * m), nn(dst[:WORDS], qws * m), nn(dst[WORDS:], qes * m))
            sums = parts if sums is None else tuple(a + b for a, b in zip(sums, parts))
            kth = kt[h * HD:(h + 1) * HD]
            dqw_parts.append(nn(kth[:, :WORDS], dst[:WORDS]))
            dqe_parts.append(nn(kth[:, WORDS:], dst[WORDS:]))
        put(0, s, n, (jnp.concatenate(dqw_parts, axis=0).T * scale).astype(BF16))
        put(1, s, n, (jnp.concatenate(dqe_parts, axis=0).T * scale).astype(BF16))
    put(2, 0, WORDS, sums[1].astype(BF16))
    put(2, WORDS, length - WORDS, sums[2].astype(BF16))
    put(3, 0, length, sums[0].astype(BF16))


def attend_back_kernel(seg, qw, qe, k, v, o, g, lse, dqw, dqe, dk, dv, bias, *, step):
    @pl.when(pl.program_id(1) == 0)
    def _():
        bias[...] = document_bias(seg[0])

    def put(slot, lo, n, value):
        (dqw, dqe, dk, dv)[slot][0, lo:lo + n] = value

    attend_back_pair(qw, qe, k, v, o, g, lse, bias, put, step)


def attend_back(qw, qe, k, v, seg, o, g, lse, step=256):
    seqs, length, width = k.shape
    pairs = width // (2 * HD)
    spec = pl.BlockSpec((1, length, 2 * HD), lambda s, h: (s, 0, h))
    out = jax.ShapeDtypeStruct((seqs, length, width), BF16)
    return pl.pallas_call(
        functools.partial(attend_back_kernel, step=step),
        grid=(seqs, pairs),
        in_specs=[
            pl.BlockSpec((1, 1, length), lambda s, h: (s, 0, 0)),
            spec, spec, spec, spec, spec, spec,
            pl.BlockSpec((1, 1, 2, length), lambda s, h: (s, h, 0, 0)),
        ],
        out_specs=[spec] * 4,
        out_shape=[out] * 4,
        scratch_shapes=[pltpu.VMEM((length, length), F32)],
        compiler_params=vmem(48),
        name="attend_back",
    )(seg[:, None, :], qw, qe, k, v, o, g, lse)


def norm_forward(values):
    center = values - jnp.mean(values, axis=-1, keepdims=True)
    scale = lax.rsqrt(jnp.mean(center * center, axis=-1, keepdims=True) + norm_eps)
    return center * scale, scale


def norm_backward(grad, normed, scale):
    first = jnp.mean(grad, axis=-1, keepdims=True)
    second = jnp.mean(grad * normed, axis=-1, keepdims=True)
    return scale * (grad - first - normed * second)


def gelu_pair(u):
    z = jnp.abs(u) * (0.5 ** 0.5)
    t = 1.0 / (1.0 + 0.3275911 * z)
    e = jnp.exp(u * u * -0.5)
    poly = 0.5 * 1.061405429
    poly = poly * t + 0.5 * -1.453152027
    poly = poly * t + 0.5 * 1.421413741
    poly = poly * t + 0.5 * -0.284496736
    poly = poly * t + 0.5 * 0.254829592
    tail = poly * t * e
    cdf = jnp.where(u < 0, tail, 1.0 - tail)
    return cdf, cdf + u * (e * 0.3989422804014327)


def colsum(v):
    return jnp.sum(v, axis=0, keepdims=True)


OUT_BIAS, GAIN_ATTN, SHIFT_ATTN, DOWN_BIAS, GAIN_FFN, SHIFT_FFN = range(6)


def middle_kernel(x, ctx, cot, wo, wi, wd, small, ib, out, gpre, hl, act, gu, gfed, gatt, gctx,
                  sums, slope, *, step):
    @pl.when(pl.program_id(0) == 0)
    def _():
        sums[...] = jnp.zeros_like(sums)

    def row(i):
        return small[6 + i:7 + i]

    ff = wi.shape[1]
    attended = nn(ctx[...], wo[...]) + row(OUT_BIAS)
    normed_attn, scale_attn = norm_forward(x[...].astype(F32) + attended)
    hidden = normed_attn * row(GAIN_ATTN) + row(SHIFT_ATTN)
    low = hidden.astype(BF16)
    hl[...] = low
    fed = jnp.broadcast_to(row(DOWN_BIAS), hidden.shape)
    for s, n in spans(ff, step):
        u = nn(low, wi[:, s:s + n]) + ib[:, s:s + n]
        cdf, grad = gelu_pair(u)
        slope[:, s:s + n] = grad
        a = (u * cdf).astype(BF16)
        act[:, s:s + n] = a
        fed = fed + nn(a, wd[s:s + n])
    normed_ffn, scale_ffn = norm_forward(hidden + fed)
    out[...] = (normed_ffn * row(GAIN_FFN) + row(SHIFT_FFN)).astype(BF16)
    gy = cot[...].astype(F32)
    sums[GAIN_FFN:GAIN_FFN + 1] += colsum(gy * normed_ffn)
    sums[SHIFT_FFN:SHIFT_FFN + 1] += colsum(gy)
    gsum = norm_backward(gy * row(GAIN_FFN), normed_ffn, scale_ffn)
    gf = gsum.astype(BF16)
    gfed[...] = gf
    sums[DOWN_BIAS:DOWN_BIAS + 1] += colsum(gf.astype(F32))
    ghid = gsum
    for s, n in spans(ff, step):
        d = nt(gf, wd[s:s + n]) * slope[:, s:s + n]
        sums[16 + s // n:17 + s // n] += colsum(d)
        d = d.astype(BF16)
        gu[:, s:s + n] = d
        ghid = ghid + nt(d, wi[:, s:s + n])
    sums[GAIN_ATTN:GAIN_ATTN + 1] += colsum(ghid * normed_attn)
    sums[SHIFT_ATTN:SHIFT_ATTN + 1] += colsum(ghid)
    gp = norm_backward(ghid * row(GAIN_ATTN), normed_attn, scale_attn)
    gpre[...] = gp
    ga = gp.astype(BF16)
    gatt[...] = ga
    sums[OUT_BIAS:OUT_BIAS + 1] += colsum(ga.astype(F32))
    gctx[...] = nt(ga, wo[...]).astype(BF16)


def middle(x, ctx, cot, wo, wi, wd, small, ib, rows=256, step=768):
    total, width = x.shape
    ff = wi.shape[1]

    def block(n):
        return pl.BlockSpec((rows, n), lambda i: (i, 0))

    def whole(*shape):
        return pl.BlockSpec(shape, lambda i: (0, 0), pipeline_mode=pl.Buffered(1))

    def out(n, dtype):
        return jax.ShapeDtypeStruct((total, n), dtype)

    return pl.pallas_call(
        functools.partial(middle_kernel, step=step),
        grid=(total // rows,),
        in_specs=[
            block(width), block(width), block(width),
            whole(width, width), whole(width, ff), whole(ff, width),
            whole(16, width), whole(1, ff),
        ],
        out_specs=[
            block(width), block(width), block(width), block(ff), block(ff),
            block(width), block(width), block(width),
            pl.BlockSpec((24, width), lambda i: (0, 0)),
        ],
        out_shape=[
            out(width, BF16), out(width, F32), out(width, BF16), out(ff, BF16), out(ff, BF16),
            out(width, BF16), out(width, BF16), out(width, BF16),
            jax.ShapeDtypeStruct((24, width), F32),
        ],
        scratch_shapes=[pltpu.VMEM((rows, ff), F32)],
        compiler_params=vmem(60),
        name="middle",
    )(x, ctx, cot, wo, wi, wd, small, ib)


def ffn_grads_kernel(hl, gu, act_lo, act_hi, gfed, ctx, gatt, dwi, dwd, dwo, hlt):
    @pl.when(pl.program_id(0) == 0)
    def _():
        hlt[...] = hl[...].T
        dwo[0] = nn(ctx[...].T, gatt[...]).astype(BF16)

    half = act_lo.shape[1]
    dwi[0] = nn(hlt[...], gu[...]).astype(BF16)
    dwd[0, :half] = nn(act_lo[...].T, gfed[...]).astype(BF16)
    dwd[0, half:] = nn(act_hi[...].T, gfed[...]).astype(BF16)


def ffn_grads(hl, gu, act, gfed, ctx, gatt):
    total, width = hl.shape
    count = gu.shape[1] // width
    half = width // 2

    def whole():
        return pl.BlockSpec((total, width), lambda j: (0, 0), pipeline_mode=pl.Buffered(1))

    square = pl.BlockSpec((1, width, width), lambda j: (j, 0, 0))
    return pl.pallas_call(
        ffn_grads_kernel,
        grid=(count,),
        in_specs=[
            whole(),
            pl.BlockSpec((total, width), lambda j: (0, j)),
            pl.BlockSpec((total, half), lambda j: (0, j)),
            pl.BlockSpec((total, half), lambda j: (0, count + j)),
            whole(), whole(), whole(),
        ],
        out_specs=[square, square, pl.BlockSpec((1, width, width), lambda j: (0, 0, 0))],
        out_shape=[
            jax.ShapeDtypeStruct((count, width, width), BF16),
            jax.ShapeDtypeStruct((count, width, width), BF16),
            jax.ShapeDtypeStruct((1, width, width), BF16),
        ],
        scratch_shapes=[pltpu.VMEM((width, total), BF16)],
        compiler_params=vmem(60),
        name="ffn_grads",
    )(hl, gu, act, act, gfed, ctx, gatt)


def input_grads_kernel(dqw, dqe, dk, dv, w, gpre, dx):
    dx[0, :WORDS] = (
        gpre[0, :WORDS] + nt(dqw[0, :WORDS], w[0]) + nt(dqe[0, :WORDS], w[1])
        + nt(dk[0, :WORDS], w[4]) + nt(dv[0, :WORDS], w[5])
    )
    dx[0, WORDS:] = (
        gpre[0, WORDS:] + nt(dqw[0, WORDS:], w[2]) + nt(dqe[0, WORDS:], w[3])
        + nt(dk[0, WORDS:], w[4]) + nt(dv[0, WORDS:], w[5])
    )


def input_grads(dqw, dqe, dk, dv, w, gpre):
    seqs, length, width = dqw.shape
    cols = 256
    full = pl.BlockSpec((1, length, width), lambda j, s: (s, 0, 0))
    part = pl.BlockSpec((1, length, cols), lambda j, s: (s, 0, j))
    return pl.pallas_call(
        input_grads_kernel,
        grid=(width // cols, seqs),
        in_specs=[full] * 4 + [pl.BlockSpec((6, cols, width), lambda j, s: (0, j, 0)), part],
        out_specs=part,
        out_shape=jax.ShapeDtypeStruct((seqs, length, width), F32),
        compiler_params=vmem(48),
        name="input_grads",
    )(dqw, dqe, dk, dv, w, gpre)


def qkv_grads_kernel(x, dqw, dqe, dk, dv, dw, sums, xt):
    seqs, length, width = x.shape

    @pl.when(pl.program_id(0) == 0)
    def _():
        for s in range(seqs):
            xt[s] = x[s].T

    def grad(source, lo, hi):
        total = nn(xt[0, :, lo:hi], source[0, lo:hi])
        for s in range(1, seqs):
            total = total + nn(xt[s, :, lo:hi], source[s, lo:hi])
        return total.astype(BF16)

    def bias(source, lo, hi):
        total = colsum(source[0, lo:hi].astype(F32))
        for s in range(1, seqs):
            total = total + colsum(source[s, lo:hi].astype(F32))
        return total

    for i, (source, lo, hi) in enumerate([
        (dqw, 0, WORDS), (dqe, 0, WORDS), (dqw, WORDS, length), (dqe, WORDS, length),
        (dk, 0, length), (dv, 0, length),
    ]):
        dw[i] = grad(source, lo, hi)
        if i != 4:
            sums[i:i + 1] = bias(source, lo, hi)


def qkv_grads(x, dqw, dqe, dk, dv, cols=256):
    seqs, length, width = x.shape
    part = pl.BlockSpec((seqs, length, cols), lambda j: (0, 0, j))
    return pl.pallas_call(
        qkv_grads_kernel,
        grid=(width // cols,),
        in_specs=[pl.BlockSpec((seqs, length, width), lambda j: (0, 0, 0), pipeline_mode=pl.Buffered(1))]
        + [part] * 4,
        out_specs=[
            pl.BlockSpec((6, width, cols), lambda j: (0, 0, j)),
            pl.BlockSpec((8, cols), lambda j: (0, j)),
        ],
        out_shape=[
            jax.ShapeDtypeStruct((6, width, width), BF16),
            jax.ShapeDtypeStruct((8, width), F32),
        ],
        scratch_shapes=[pltpu.VMEM((seqs, width, length), BF16)],
        compiler_params=vmem(60),
        name="qkv_grads",
    )(x, dqw, dqe, dk, dv)

MESH = pl.DeviceIdType.MESH
UNIT = 384


def place():
    d = lax.axis_index("dp")
    f = lax.axis_index("fsdp")
    bits = {"core": d % 2, "y": (d // 2) % 2, "z0": (d // 4) % 2, "z1": (d // 8) % 2, "x": f}
    peers = {"x": {"fsdp": 1 - f}}
    for name, size in (("core", 1), ("y", 2), ("z0", 4), ("z1", 8)):
        peers[name] = {"dp": d + size - 2 * size * bits[name]}
    return bits, peers


def greet(peers, names):
    barrier = pltpu.get_barrier_semaphore()
    for name in names:
        pl.semaphore_signal(barrier, inc=1, device_id=peers[name], device_id_type=MESH)
    pl.semaphore_wait(barrier, len(names))


def gather_project_kernel(*refs, units):
    own = refs[:9]
    small, x = refs[9:11]
    w6, wo, wi, wd, wide, ib, qw, qe, keys, vals, xt = refs[11:22]
    wv, table, qv, xt_held, send, recv, local, small_sem, q_sem = refs[22:]
    bits, peers = place()
    f, c = bits["x"], bits["core"]
    piece = UNIT // 8
    n = len(units)
    seqs, length, width = x.shape

    def load(u):
        i, kind, k = units[u]
        if kind == "wi":
            src = own[i].at[:, k * width:(k + 1) * width]
        else:
            src = own[i].at[k * UNIT:(k + 1) * UNIT]
        return pltpu.make_async_copy(src, wv.at[u, f], local.at[u])

    def store(u):
        i, kind, k = units[u]
        if kind == "w6":
            dst = w6.at[i]
        elif kind == "wo":
            dst = wo
        elif kind == "wi":
            dst = wi.at[:, :, k * width:(k + 1) * width]
        else:
            dst = wd.at[:, k]
        return pltpu.make_async_copy(wv.at[u], dst, local.at[u])

    small_in = pltpu.make_async_copy(small, table.at[f], small_sem.at[2])
    small_in.start()
    for u in range(n):
        load(u).start()
    greet(peers, ("x", "y", "z0", "core"))

    def remote(u, stage, half, rows, size, peer):
        here = wv.at[u, half, pl.ds(pl.multiple_of(rows, 16), size)]
        return pltpu.make_async_remote_copy(
            src_ref=here, dst_ref=here, send_sem=send.at[u, stage], recv_sem=recv.at[u, stage],
            device_id=peers[peer], device_id_type=MESH,
        )

    def copy(u, stage):
        first, second = ("y", "z0") if u % 2 == 0 else ("z0", "y")
        a, b = bits[first], bits[second]
        mine = (c * 4 + b * 2 + a) * piece
        pair = (c * 4 + b * 2) * piece
        away = (c * 4 + (1 - b) * 2) * piece
        if stage == 0:
            return remote(u, 0, f, mine, piece, "x")
        if stage == 1:
            return remote(u, 1, 1 - f, mine, piece, first)
        if stage == 2:
            return remote(u, 2, 1 - f, pair, 2 * piece, second)
        return remote(u, stage, 1 - f, pair if stage == 3 else away, 2 * piece, "core")

    small_in.wait()
    small_copy = pltpu.make_async_remote_copy(
        src_ref=table.at[f], dst_ref=table.at[f], send_sem=small_sem.at[0], recv_sem=small_sem.at[1],
        device_id=peers["x"], device_id_type=MESH,
    )
    small_copy.start()
    for u in range(n):
        load(u).wait()
        copy(u, 0).start()

    def fill_small():
        small_copy.wait_recv()
        half = table.shape[2]
        for s in range(2):
            wide[:, s * half:(s + 1) * half] = table[s].astype(F32)
            for r in range(4):
                ib[:, (4 * s + r) * half:(4 * s + r + 1) * half] = table[s, 12 + r:13 + r].astype(F32)

    cols = 256
    scale = HD ** -0.5

    def project(i):
        lo, hi = ((0, WORDS), (0, WORDS), (WORDS, length), (WORDS, length), (0, length), (0, length))[i]
        slot = (0, 1, 0, 1, 2, 3)[i]

        def tile(j, carry):
            at = pl.ds(pl.multiple_of(j * cols, cols), cols)
            w = wv[i, :, :, at].reshape(width, cols)
            for s in range(seqs):
                total = nn(x[s, lo:hi], w)
                if i != 4:
                    total = total + wide[i:i + 1, at]
                total = total.astype(BF16)
                if i < 4:
                    total = (total * scale).astype(BF16)
                qv[slot, s, lo:hi, at] = total
            return carry

        lax.fori_loop(0, width // cols, tile, 0)

    xt_out = pltpu.make_async_copy(xt_held, xt, q_sem.at[4])

    def q_out(slot):
        return pltpu.make_async_copy(qv.at[slot], (qw, qe, keys, vals)[slot], q_sem.at[slot])

    lag1, lag2, lag3 = 2, 4, 5
    for t in range(n + lag3):
        if t < n:
            copy(t, 0).wait_recv()
            copy(t, 1).start()
        if 0 <= t - lag1 < n:
            copy(t - lag1, 1).wait_recv()
            copy(t - lag1, 2).start()
            copy(t - lag1, 3).start()
        if 0 <= t - lag2 < n:
            copy(t - lag2, 2).wait_recv()
            copy(t - lag2, 4).start()
        if t == 1:
            for s in range(seqs):
                xt_held[s] = x[s].T
            xt_out.start()
        if t == 2:
            fill_small()
        done = t - lag3
        if 0 <= done < n:
            copy(done, 3).wait_recv()
            copy(done, 4).wait_recv()
            store(done).start()
        if 0 <= done < 6:
            project(done)
            if done >= 2:
                q_out(done - 2).start()
    for u in range(n):
        for stage in range(5):
            copy(u, stage).wait_send()
        store(u).wait()
    small_copy.wait_send()
    for slot in range(4):
        q_out(slot).wait()
    xt_out.wait()


def gather_project(own, small, x):
    units = [(i, "w6", 0) for i in range(6)] + [(6, "wo", 0)]
    for k in range(4):
        units += [(7, "wi", k), (8, "wd", k)]
    n = len(units)
    seqs, length, width = x.shape
    ff = own[7].shape[1]
    hbm = pl.BlockSpec(memory_space=pltpu.MemorySpace.HBM)
    vm = pl.BlockSpec(memory_space=pltpu.VMEM)
    q = jax.ShapeDtypeStruct(x.shape, BF16)
    w6, wo, wi, wd, wide, ib, qw, qe, keys, vals, xt = pl.pallas_call(
        functools.partial(gather_project_kernel, units=units),
        in_specs=[hbm] * 10 + [vm],
        out_specs=[hbm] * 4 + [vm] * 2 + [hbm] * 5,
        out_shape=[
            jax.ShapeDtypeStruct((6, 2, UNIT, width), BF16),
            jax.ShapeDtypeStruct((2, UNIT, width), BF16),
            jax.ShapeDtypeStruct((2, UNIT, ff), BF16),
            jax.ShapeDtypeStruct((2, 4, UNIT, width), BF16),
            jax.ShapeDtypeStruct((16, width), F32),
            jax.ShapeDtypeStruct((1, ff), F32),
            q, q, q, q,
            jax.ShapeDtypeStruct((seqs, width, length), BF16),
        ],
        scratch_shapes=[
            pltpu.VMEM((n, 2, UNIT, width), BF16),
            pltpu.VMEM((2,) + small.shape, small.dtype),
            pltpu.VMEM((4,) + x.shape, BF16),
            pltpu.VMEM((seqs, width, length), BF16),
            pltpu.SemaphoreType.DMA((n, 5)),
            pltpu.SemaphoreType.DMA((n, 5)),
            pltpu.SemaphoreType.DMA((n,)),
            pltpu.SemaphoreType.DMA((3,)),
            pltpu.SemaphoreType.DMA((5,)),
        ],
        compiler_params=pltpu.CompilerParams(
            collective_id=0, has_side_effects=True, vmem_limit_bytes=60 * 1024 * 1024
        ),
        name="gather_project",
    )(*own, small, x)
    return (w6.reshape(6, width, width), wo.reshape(width, width), wi.reshape(width, ff),
            wd.reshape(ff, width), wide, ib, qw, qe, keys, vals, xt)


def widen_kernel(g, *refs):
    outs = refs[:9]
    stage, sem = refs[9:]
    n = g.shape[0]
    width = g.shape[2]
    slots = stage.shape[0]

    def out(u):
        if u < 4:
            dst = outs[0].at[:, u * width:(u + 1) * width]
        elif u < 8:
            dst = outs[1].at[(u - 4) * UNIT:(u - 3) * UNIT]
        else:
            dst = outs[u - 6]
        return pltpu.make_async_copy(stage.at[u % slots], dst, sem.at[u % slots])

    for u in range(n):
        if u >= slots:
            out(u - slots).wait()
        stage[u % slots] = g[u].astype(F32)
        out(u).start()
    for u in range(n - slots, n):
        out(u).wait()


def widen(g):
    n, share, width = g.shape
    hbm = pl.BlockSpec(memory_space=pltpu.MemorySpace.HBM)
    square = jax.ShapeDtypeStruct((share, width), F32)
    return pl.pallas_call(
        widen_kernel,
        in_specs=[pl.BlockSpec(memory_space=pltpu.VMEM)],
        out_specs=[hbm] * 9,
        out_shape=[
            jax.ShapeDtypeStruct((share, 4 * width), F32),
            jax.ShapeDtypeStruct((4 * share, width), F32),
        ] + [square] * 7,
        scratch_shapes=[pltpu.VMEM((4, share, width), F32), pltpu.SemaphoreType.DMA((4,))],
        compiler_params=vmem(60),
        name="widen",
    )(g)


STAGES = ("core", "x", "y", "z0", "z1")
PAIRS_END = 12
UNITS_END = 18
STEPS = 24


class Reduction:
    def __init__(self, own, from_core, from_x, from_y, from_z0, from_z1, full, send, recv, peers, bits):
        self.own, self.full = own, full
        self.got = (from_core, from_x, from_y, from_z0, from_z1)
        self.send, self.recv, self.peers = send, recv, peers
        f = self.f = bits["x"]
        self.mine = pl.multiple_of(bits["core"] * UNIT, UNIT)
        self.theirs = pl.multiple_of((1 - bits["core"]) * UNIT, UNIT)
        y0 = self.y0 = bits["y"] * 192
        z0 = self.z0 = y0 + bits["z0"] * 96
        z1 = self.z1 = z0 + bits["z1"] * 48
        away = {
            1: ((1 - f) * UNIT, UNIT),
            2: (f * UNIT + (1 - bits["y"]) * 192, 192),
            3: (f * UNIT + y0 + (1 - bits["z0"]) * 96, 96),
            4: (f * UNIT + z0 + (1 - bits["z1"]) * 48, 48),
        }
        self.away = away
        self.back = {5: (z1, 48, "z1"), 6: (z0, 96, "z0"), 7: (y0, 192, "y"), 8: (0, UNIT, "core")}

    def rows(self, start, size):
        return pl.ds(pl.multiple_of(start, 16), size)

    def remote(self, u, stage, src, dst, peer):
        return pltpu.make_async_remote_copy(
            src_ref=src, dst_ref=dst, send_sem=self.send.at[u, stage], recv_sem=self.recv.at[u, stage],
            device_id=self.peers[peer], device_id_type=MESH,
        )

    def first(self, u, unit):
        return self.remote(u, 0, unit.at[:, pl.ds(self.theirs, UNIT)], self.got[0].at[u], "core")

    def copy(self, u, stage):
        if stage < 5:
            start, size = self.away[stage]
            src = self.own.at[u, self.rows(start, size)]
            return self.remote(u, stage, src, self.got[stage].at[u], STAGES[stage])
        start, size, peer = self.back[stage]
        here = self.full.at[u, self.rows(start, size), pl.ds(self.mine, UNIT)]
        return self.remote(u, stage, here, here, peer)

    def add(self, u, start, size, got):
        here = self.rows(start, size)
        self.own[u, here] = (self.own[u, here].astype(F32) + got.astype(F32)).astype(BF16)

    def after(self, u, stage):
        f = self.f
        if stage < 4:
            self.copy(u, stage).wait_recv()
            start, size = {1: (0, UNIT), 2: (self.y0, 192), 3: (self.z0, 96)}[stage]
            self.add(u, f * UNIT + start, size, self.got[stage][u])
            self.copy(u, stage + 1).start()
        elif stage == 4:
            self.copy(u, 4).wait_recv()
            here = self.rows(f * UNIT + self.z1, 48)
            self.full[u, self.rows(self.z1, 48), pl.ds(self.mine, UNIT)] = (
                self.own[u, here].astype(F32) + self.got[4][u].astype(F32)
            ).astype(BF16)
            self.copy(u, 5).start()
        elif stage < 8:
            self.copy(u, stage).wait_recv()
            self.copy(u, stage + 1).start()
        else:
            self.copy(u, 8).wait_recv()


LAGS = {1: 2, 2: 3, 3: 4, 4: 5, 5: 6, 6: 7, 7: 8, 8: 9}
SMALL_FROM = 10


def backward_kernel(seg, qw, qe, k, v, o, g, lse, xt, w6, gpre, gi, gd, go, small_in,
                    dx, out, small_out,
                    bias, grads, unit, full, own, from_core, from_x, from_y, from_z0, from_z1,
                    small_sum, small_got, send, recv, local, small_send, small_recv, *, step):
    i = pl.program_id(0)
    bits, peers = place()
    red = Reduction(own, from_core, from_x, from_y, from_z0, from_z1, full, send, recv, peers, bits)
    ready = gi.shape[0] + gd.shape[0] + go.shape[0]
    total = ready + 6
    seqs = xt.shape[0]
    width = xt.shape[1]
    length = xt.shape[2]
    sources = ((gi, 0), (gd, gi.shape[0]), (go, gi.shape[0] + gd.shape[0]))

    def load(g, n, u):
        return pltpu.make_async_copy(g.at[n, :, pl.ds(red.mine, UNIT)], own.at[u], local.at[u])

    def out_copy(u):
        return pltpu.make_async_copy(full.at[u], out.at[u], local.at[u])

    def small_copy(s):
        return pltpu.make_async_remote_copy(
            src_ref=small_sum.at[s], dst_ref=small_got.at[s], send_sem=small_send.at[s],
            recv_sem=small_recv.at[s], device_id=peers[STAGES[s]], device_id_type=MESH,
        )

    @pl.when(i == 0)
    def _():
        greet(peers, STAGES)
        small_sum[0] = small_in[...]
        for source, base in sources:
            def begin(n, carry, source=source, base=base):
                red.first(base + n, source.at[n]).start()
                load(source, n, base + n).start()
                return carry
            lax.fori_loop(0, source.shape[0], begin, 0)

    def comm_step(t, carry):
        @pl.when(t < total)
        def _():
            red.first(t, gi.at[0]).wait_recv()

            @pl.when(t < ready)
            def _():
                load(gi, 0, t).wait()
            for n in range(2):
                red.add(t, n * UNIT, UNIT, from_core[t, n * UNIT:(n + 1) * UNIT])
            red.copy(t, 1).start()

        for stage, lag in LAGS.items():
            @pl.when(jnp.logical_and(t >= lag, t < total + lag))
            def _(stage=stage, lag=lag):
                red.after(t - lag, stage)
                if stage == 8:
                    out_copy(t - lag).start()

        for s in range(5):
            @pl.when(t == SMALL_FROM + s)
            def _(s=s):
                small_copy(s).wait_recv()
                value = small_sum[s] + small_got[s]
                if s < 4:
                    small_sum[s + 1] = value
                    small_copy(s + 1).start()
                else:
                    small_out[...] = value
        return carry

    @pl.when(jnp.logical_and(i < PAIRS_END, i % 6 == 0))
    def _():
        bias[...] = document_bias(seg[0])

    @pl.when(i < PAIRS_END)
    def _():
        s = i // 6
        at = pl.ds(pl.multiple_of((i % 6) * 2 * HD, 2 * HD), 2 * HD)

        def put(slot, lo, n, value):
            grads[slot, s, pl.ds(lo, n), at] = value

        attend_back_pair(qw, qe, k, v, o, g, lse, bias, put, step)

    for n in range(6):
        @pl.when(i == PAIRS_END + n)
        def _(n=n):
            u = ready + n
            slot = (0, 1, 0, 1, 2, 3)[n]
            lo, hi = ((0, WORDS), (0, WORDS), (WORDS, length), (WORDS, length), (0, length), (0, length))[n]
            buf = unit.at[n % 2]
            if n >= 2:
                red.first(u - 2, buf).wait_send()

            def tile(j, carry):
                cols = pl.ds(pl.multiple_of(j * 256, 256), 256)
                value = nn(xt[0, :, lo:hi], grads[slot, 0, lo:hi, cols])
                for s in range(1, seqs):
                    value = value + nn(xt[s, :, lo:hi], grads[slot, s, lo:hi, cols])
                buf[:, cols] = value.astype(BF16)
                if n != 4:
                    column = colsum(grads[slot, 0, lo:hi, cols].astype(F32))
                    for s in range(1, seqs):
                        column = column + colsum(grads[slot, s, lo:hi, cols].astype(F32))
                    small_sum[0, 8 + n:9 + n, cols] = column
                return carry

            lax.fori_loop(0, width // 256, tile, 0)
            red.first(u, buf).start()
            own[u] = buf[:, pl.ds(red.mine, UNIT)]
            if n == 5:
                small_copy(0).start()

    @pl.when(i >= UNITS_END)
    def _():
        s = i % 2

        def grad(slot, lo, hi, n):
            return nt(grads[slot, s, lo:hi], w6[n])

        for lo, hi, a, b in ((0, WORDS, 0, 1), (WORDS, length, 2, 3)):
            dx[0, lo:hi] = (
                gpre[0, lo:hi] + grad(0, lo, hi, a) + grad(1, lo, hi, b)
                + grad(2, lo, hi, 4) + grad(3, lo, hi, 5)
            )

    @pl.when(i % 2 == 1)
    def _():
        comm_step(i // 2, 0)

    @pl.when(i == STEPS - 1)
    def _():
        lax.fori_loop(STEPS // 2, total + 9, comm_step, 0)

        def drain(u, carry):
            @pl.when(jnp.logical_or(u < ready, u >= ready + 4))
            def _():
                red.first(u, gi.at[0]).wait_send()
            for stage in range(1, 9):
                red.copy(u, stage).wait_send()
            out_copy(u).wait()
            return carry

        lax.fori_loop(0, total, drain, 0)
        for s in range(5):
            small_copy(s).wait_send()


def backward(qw, qe, k, v, seg, o, g, lse, xt, w6, gpre, units, small, step=256):
    seqs, length, width = k.shape
    gi, gd, go = units
    total = gi.shape[0] + gd.shape[0] + go.shape[0] + 6
    hbm = pl.BlockSpec(memory_space=pltpu.MemorySpace.HBM)
    vm = pl.BlockSpec(memory_space=pltpu.VMEM)

    def pair(i):
        return jnp.minimum(i, PAIRS_END - 1)

    def late(i):
        return jnp.maximum(i - UNITS_END, 0)

    spec = pl.BlockSpec((1, length, 2 * HD), lambda i: (pair(i) // 6, 0, pair(i) % 6))
    part = pl.BlockSpec((1, length, 256), lambda i: (late(i) % 2, 0, late(i) // 2))
    return pl.pallas_call(
        functools.partial(backward_kernel, step=step),
        grid=(STEPS,),
        in_specs=[
            pl.BlockSpec((1, 1, length), lambda i: (pair(i) // 6, 0, 0)),
            spec, spec, spec, spec, spec, spec,
            pl.BlockSpec((1, 1, 2, length), lambda i: (pair(i) // 6, pair(i) % 6, 0, 0)),
            pl.BlockSpec((seqs, width, length), lambda i: (0, 0, 0), pipeline_mode=pl.Buffered(1)),
            pl.BlockSpec((6, 256, width), lambda i: (0, late(i) // 2, 0), pipeline_mode=pl.Buffered(1)),
            part, hbm, hbm, hbm,
            pl.BlockSpec(small.shape, lambda i: (0, 0), pipeline_mode=pl.Buffered(1)),
        ],
        out_specs=[part, hbm, vm],
        out_shape=[
            jax.ShapeDtypeStruct((seqs, length, width), F32),
            jax.ShapeDtypeStruct((total, UNIT, width), BF16),
            jax.ShapeDtypeStruct(small.shape, F32),
        ],
        scratch_shapes=[
            pltpu.VMEM((length, length), F32),
            pltpu.VMEM((4, seqs, length, width), BF16),
            pltpu.VMEM((2, width, width), BF16),
            pltpu.VMEM((total, UNIT, width), BF16),
            pltpu.VMEM((total, 2 * UNIT, UNIT), BF16),
            pltpu.VMEM((total, 2 * UNIT, UNIT), BF16),
            pltpu.VMEM((total, 384, UNIT), BF16),
            pltpu.VMEM((total, 192, UNIT), BF16),
            pltpu.VMEM((total, 96, UNIT), BF16),
            pltpu.VMEM((total, 48, UNIT), BF16),
            pltpu.VMEM((5,) + small.shape, F32),
            pltpu.VMEM((5,) + small.shape, F32),
            pltpu.SemaphoreType.DMA((total, 9)),
            pltpu.SemaphoreType.DMA((total, 9)),
            pltpu.SemaphoreType.DMA((total,)),
            pltpu.SemaphoreType.DMA((5,)),
            pltpu.SemaphoreType.DMA((5,)),
        ],
        compiler_params=pltpu.CompilerParams(
            collective_id=1, has_side_effects=True, vmem_limit_bytes=67043328,
        ),
        name="backward",
    )(seg[:, None, :], qw, qe, k, v, o, g, lse, xt, w6, gpre, gi, gd, go, small)


def local(
    inputs, segments,
    query_wordword, query_wordent, query_entword, query_entent,
    bias_wordword, bias_wordent, bias_entword, bias_entent,
    key_weight, value_weight, value_bias, out_weight, out_bias,
    gain_attn, shift_attn, inner_weight, inner_bias, down_weight, down_bias,
    gain_ffn, shift_ffn, cotangent, *, dp, fsdp,
):
    seqs, length, width = inputs.shape
    share = width // fsdp
    ff = inner_weight.shape[1]
    paired = dp == 16 and fsdp == 2

    def gather_all(value):
        return lax.all_gather(value, "fsdp", axis=0, tiled=True)

    vectors = {
        0: bias_wordword, 1: bias_wordent, 2: bias_entword, 3: bias_entent, 5: value_bias,
        6: out_bias, 7: gain_attn, 8: shift_attn, 9: down_bias, 10: gain_ffn, 11: shift_ffn,
    }
    for n in range(4):
        vectors[12 + n] = inner_bias[n * share:(n + 1) * share]
    place_row = lax.broadcasted_iota(jnp.int32, (16, share), 0)
    packed = jnp.zeros((16, share), BF16)
    for n, vector in vectors.items():
        packed = jnp.where(place_row == n, vector[None, :], packed)
    own = (query_wordword, query_wordent, query_entword, query_entent, key_weight, value_weight,
           out_weight, inner_weight, down_weight)
    if paired:
        w6, wo, wi, wd, wide, ib, qw, qe, keys, vals, xt = gather_project(own, packed, inputs)
    else:
        w6 = jnp.stack([gather_all(w) for w in own[:6]])
        wo, wi, wd = [gather_all(w) for w in own[6:]]
        table = lax.all_gather(packed, "fsdp", axis=0)
        wide = table.transpose(1, 0, 2).reshape(16, width).astype(F32)
        ib = table[:, 12:].reshape(1, ff).astype(F32)
        qw, qe, keys, vals = project(inputs, w6, wide)
    ctx, lse = attend(qw, qe, keys, vals, segments)

    def flat(value):
        return value.reshape(seqs * length, width)

    ctx_rows = flat(ctx)
    out, gpre, hl, act, gu, gfed, gatt, gctx, sums = middle(
        flat(inputs), ctx_rows, flat(cotangent), wo, wi, wd, wide, ib)
    units = ffn_grads(hl, gu, act, gfed, ctx_rows, gatt)
    gctx = gctx.reshape(inputs.shape)
    gpre = gpre.reshape(inputs.shape)
    f = lax.axis_index("fsdp")

    if paired:
        grad_inputs, grads, totals = backward(
            qw, qe, keys, vals, segments, ctx, gctx, lse, xt, w6, gpre, units, sums)
        g_wi, g_wd, g_wo, *g6 = widen(grads)
    else:
        dqw, dqe, dk, dv = attend_back(qw, qe, keys, vals, segments, ctx, gctx, lse)
        grad_inputs = input_grads(dqw, dqe, dk, dv, w6, gpre)
        dw6, qsums = qkv_grads(inputs, dqw, dqe, dk, dv)

        def shared(grad):
            part = lax.psum_scatter(grad, "fsdp", scatter_dimension=0, tiled=True)
            return lax.psum(part, "dp").astype(F32)

        g_wi = shared(units[0].transpose(1, 0, 2).reshape(width, ff))
        g_wd = shared(units[1].reshape(4, 2, width // 2, width).transpose(1, 0, 2, 3).reshape(ff, width))
        g_wo = shared(units[2][0])
        g6 = [shared(dw6[i]) for i in range(6)]
        totals = lax.psum(jnp.concatenate([sums[:8], qsums, sums[16:]]), ("dp", "fsdp"))

    mine = lax.dynamic_slice_in_dim(totals[:16], f * share, share, axis=1)
    g_ib = lax.dynamic_slice_in_dim(totals[16:20].reshape(ff), f * (ff // fsdp), ff // fsdp)
    return (
        out.reshape(inputs.shape), grad_inputs,
        g6[0], g6[1], g6[2], g6[3],
        mine[8], mine[9], mine[10], mine[11],
        g6[4], g6[5], mine[13],
        g_wo, mine[OUT_BIAS], mine[GAIN_ATTN], mine[SHIFT_ATTN],
        g_wi, g_ib, g_wd, mine[DOWN_BIAS], mine[GAIN_FFN], mine[SHIFT_FFN],
    )


def solution(mesh):
    rows = P(("dp", "fsdp"), None, None)
    mat = P("fsdp", None)
    vec = P("fsdp")
    params = (mat,) * 4 + (vec,) * 4 + (mat, mat, vec, mat, vec, vec, vec, mat, vec, mat, vec, vec, vec)
    return jax.shard_map(
        functools.partial(local, dp=mesh.shape["dp"], fsdp=mesh.shape["fsdp"]),
        mesh=mesh,
        in_specs=(rows, P(("dp", "fsdp"), None)) + params + (rows,),
        out_specs=(rows, rows) + params,
        check_vma=False,
    )
```

time: 462 us -> 332 us (0.72)
  Pallas kernels: 390 us -> 318 us
  local copies, waits for them, and re-layouts: 56.5 us -> 11.5 us
  other arithmetic: 13.6 us -> 1.65 us
    pallas_call x6 -> x3, Pallas kernels: 278 us -> 212 us  [the longest x1 146 us: backward(): pl.pallas_call(functools.partial(backward_kernel, step=step), grid=(STEPS...]
    unnamed x41 -> x15, local copies, waits for them, and re-layouts: 21.4 us -> 9.31 us
    convert_element_type x3 -> x0, other arithmetic: 11.5 us -> none  [the longest x1 11.5 us: local(): grads = grads.astype(F32)]
    transpose x2 -> x0, local copies, waits for them, and re-layouts: 10.9 us -> none  [local(): g_wi = grads[:4].transpose(1, 0, 2).reshape(share, ff)]
    another operation x12 -> x0, local copies, waits for them, and re-layouts: 7.53 us -> none  [local(): jnp.stack([bias_wordword, bias_wordent, bias_entword, bias_entent, zero,...]
    squeeze x1 -> x0, local copies, waits for them, and re-layouts: 6.76 us -> none  [local(): g_wo = grads[8]]
    pallas_call x1, Pallas kernels: 58.8 us -> 52.5 us  [middle(): pl.pallas_call(functools.partial(middle_kernel, step=step), grid=(total /...]
where the time goes in v2:
time: 332 us
  Pallas kernels  318 us (96%)
  local copies, waits for them, and re-layouts  11.5 us (3%)
    pallas_call x1, Pallas kernels, backward(): pl.pallas_call(functools.partial(backward_kernel, step=step), grid=(STEPS...  146 us
    pallas_call x1, Pallas kernels, gather_project(): pl.pallas_call(functools.partial(gather_project_kernel, units=units), in_...  56 us
    pallas_call x1, Pallas kernels, middle(): pl.pallas_call(functools.partial(middle_kernel, step=step), grid=(total /...  52.5 us
    pallas_call x1, Pallas kernels, attend(): pl.pallas_call(functools.partial(attend_kernel, step=step), grid=(seqs, p...  32.9 us
    pallas_call x1, Pallas kernels, ffn_grads(): pl.pallas_call(ffn_grads_kernel, grid=(count,), in_specs=[whole(), pl.Blo...  20.8 us
    pallas_call x1, Pallas kernels, widen(): pl.pallas_call(widen_kernel, in_specs=[pl.BlockSpec(memory_space=pltpu.VM...  9.77 us
    unnamed x15, local copies, waits for them, and re-layouts  9.31 us

profile of v2, /device:TPU:1, one launch (start us, length us, event | category | flops | bytes accessed | tf_op | source)
XLA Modules:
  0.0 332.0 jit_solution(8510478781565760868)
XLA Ops:
  0.7 0.8 fusion
  1.5 1.6 select_select_fusion.refs_9_
  3.1 0.0 copy-start.6
  3.2 56.0 %gather_project.1 = (bf16[6,2,384,768]{3,2,1,0:T(8,128)(2,1)}, bf16[2,384,768]{2,1,0:T(8,128)(2,1)}, bf16[2,384,3072]{2,1,0:T(8,128)(2,1)}, bf16[2,4,384,768]{3,...) custom-call(bf16[384,768]{1,0:T(8,128)(2,1)} %refs_0_.1, ...), custom_call_target="tpu_custom_call" | custom-call | tf_op jit(solution)/shard_map/gather_project/pallas_call | solution.py:602
  59.2 0.0 copy-done.6
  59.2 0.0 copy-start.1
  59.2 1.5 copy-done.1
  60.7 0.0 copy-start.2
  60.7 1.5 copy-done.2
  62.3 0.0 copy-start.4
  62.3 32.9 %attend.1 = (bf16[2,640,768]{2,1,0:T(8,128)(2,1)S(1)}, f32[2,6,2,640]{3,2,1,0:T(2,128)S(1)}) custom-call(s32[2,1,640]{2,1,0:T(1,128)S(1)} %broadcast_in_dim.100.seg, bf16[2,640,768]{2,1,0:T(8,128)(2,1)S(1)} %copy-done.1, bf16[2,640,768]{2,1,0:T(8,128)(2,1)S(1)} %copy-done.2, bf16[2,640,768]{2,1,0:T(8,128)(2,1)} %get-tuple-element.62.k, ...), custom_call_target="tpu_custom_call" | custom-call | tf_op jit(solution)/shard_map/attend/pallas_call | solution.py:108
  95.2 0.0 copy-done.4
  95.2 0.0 copy-start
  95.3 1.3 copy-done
  96.6 0.0 copy-start.3
  96.6 0.6 copy-done.3
  97.2 52.5 %middle.1 = (bf16[1280,768]{1,0:T(8,128)(2,1)}, f32[1280,768]{1,0:T(8,128)}, bf16[1280,768]{1,0:T(8,128)(2,1)}, bf16[1280,3072]{1,0:T(8,128)(2,1)}, bf16[1280,30...) custom-call(bf16[1280,768]{1,0:T(8,128)(2,1)} %bitcast.12, ...), custom_call_target="tpu_custom_call" | custom-call | tf_op jit(solution)/shard_map/middle/pallas_call | solution.py:287
  149.7 20.8 %ffn_grads.1 = (bf16[4,768,768]{2,1,0:T(8,128)(2,1)}, bf16[4,768,768]{2,1,0:T(8,128)(2,1)}, bf16[1,768,768]{2,1,0:T(8,128)(2,1)}) custom-call(bf16[1280,768]{1,0:T(8,128)(2,1)} %get-tuple-element.76.hl, bf16[1280,3072]{1,0:T(8,128)(2,1)} %get-tuple-element.77.gu, bf16[1280,3072]{1,0:T(8,128)(2,1)} %get-tuple-element.78.act_lo.act_hi, ...), custom_call_target="tpu_custom_call" | custom-call | tf_op jit(solution)/shard_map/ffn_grads/pallas_call | solution.py:332
  170.5 146.0 %backward.1 = (f32[2,640,768]{2,1,0:T(8,128)}, bf16[15,384,768]{2,1,0:T(8,128)(2,1)}, f32[24,768]{1,0:T(8,128)}) custom-call(s32[2,1,640]{2,1,0:T(1,128)} %copy-done.4, bf16[2,640,768]{2,1,0:T(8,128)(2,1)} %get-tuple-element.60.qw, bf16[2,640,768]{2,1,0:T(8,128)(2,1)} %get-tuple-element.61.qe, bf16[2,640,768]{2,1,0:T(8,128)(2,1)} %get-tuple-element.62.k, ...), custom_call_target="tpu_custom_call" | custom-call | tf_op jit(solution)/shard_map/backward/pallas_call | solution.py:916
  316.5 0.0 copy-start.5
  316.5 9.8 %widen.1 = (f32[384,3072]{1,0:T(8,128)}, f32[1536,768]{1,0:T(8,128)}, f32[384,768]{1,0:T(8,128)}, f32[384,768]{1,0:T(8,128)}, f32[384,768]{1,0:T(8,128)}, /*inde...) custom-call(bf16[15,384,768]{2,1,0:T(8,128)(2,1)} %get-tuple-element.86.g), custom_call_target="tpu_custom_call" | custom-call | tf_op jit(solution)/shard_map/widen/pallas_call | solution.py:665
  326.3 0.0 copy-done.5
  326.3 0.7 dynamic-slice_reduce_fusion
  327.0 0.7 dynamic_slice.7
  327.7 4.3 %copy.48 = f32[2,640,768]{2,1,0:T(8,128)} copy(f32[2,640,768]{2,1,0:T(8,128)} %get-tuple-element.150) | data formatting | bytes 7864320
  (12 shorter events, 0.1 us)
Async XLA Ops:
  3.1 56.0 %copy-start.6 = (s32[2,640]{1,0:T(2,128)S(1)}, s32[2,640]{1,0:T(2,128)}, u32[]{:S(2)}) copy-start(s32[2,640]{1,0:T(2,128)} %param.25) | copy-start | bytes 15364
  59.2 1.5 copy-start.1
  60.7 1.5 copy-start.2
  62.3 32.9 %copy-start.4 = (s32[2,1,640]{2,1,0:T(1,128)}, s32[2,1,640]{2,1,0:T(1,128)S(1)}, u32[]{:S(2)}) copy-start(s32[2,1,640]{2,1,0:T(1,128)S(1)} %broadcast_in_dim.100.seg) | copy-start | bytes 15364
  95.2 1.3 copy-start
  96.6 0.6 copy-start.3
  316.5 9.8 %copy-start.5 = (f32[24,768]{1,0:T(8,128)S(1)}, f32[24,768]{1,0:T(8,128)}, u32[]{:S(2)}) copy-start(f32[24,768]{1,0:T(8,128)} %get-tuple-element.91) | copy-start | bytes 221188

commit v3 on v2

--- a/solution.py
+++ b/solution.py
@@ -101,7 +101,7 @@
         o[0, s:s + n] = jnp.concatenate(parts, axis=0).T.astype(BF16)
 
 
-def attend(qw, qe, k, v, seg, step=256):
+def attend(qw, qe, k, v, seg, step=640):
     seqs, length, width = k.shape
     pairs = width // (2 * HD)
     spec = pl.BlockSpec((1, length, 2 * HD), lambda s, h: (s, 0, h))

time: 332 us -> 321 us (0.967)
  Pallas kernels: 318 us -> 307 us
    pallas_call x1, Pallas kernels: 32.9 us -> 21.8 us  [attend(): pl.pallas_call(functools.partial(attend_kernel, step=step), grid=(seqs, p...]
where the time goes in v3:
time: 321 us
  Pallas kernels  307 us (96%)
  local copies, waits for them, and re-layouts  11.5 us (4%)
    pallas_call x1, Pallas kernels, backward(): pl.pallas_call(functools.partial(backward_kernel, step=step), grid=(STEPS...  146 us
    pallas_call x1, Pallas kernels, gather_project(): pl.pallas_call(functools.partial(gather_project_kernel, units=units), in_...  56 us
    pallas_call x1, Pallas kernels, middle(): pl.pallas_call(functools.partial(middle_kernel, step=step), grid=(total /...  52.5 us
    pallas_call x1, Pallas kernels, attend(): pl.pallas_call(functools.partial(attend_kernel, step=step), grid=(seqs, p...  21.8 us
    pallas_call x1, Pallas kernels, ffn_grads(): pl.pallas_call(ffn_grads_kernel, grid=(count,), in_specs=[whole(), pl.Blo...  20.8 us
    pallas_call x1, Pallas kernels, widen(): pl.pallas_call(widen_kernel, in_specs=[pl.BlockSpec(memory_space=pltpu.VM...  9.77 us
    unnamed x15, local copies, waits for them, and re-layouts  9.31 us

profile of v3, /device:TPU:1, one launch (start us, length us, event | category | flops | bytes accessed | tf_op | source)
XLA Modules:
  0.0 320.8 jit_solution(12989216493973141693)
XLA Ops:
  0.7 0.8 fusion
  1.5 1.6 select_select_fusion.refs_9_
  3.1 0.0 copy-start.6
  3.2 56.0 %gather_project.1 = (bf16[6,2,384,768]{3,2,1,0:T(8,128)(2,1)}, bf16[2,384,768]{2,1,0:T(8,128)(2,1)}, bf16[2,384,3072]{2,1,0:T(8,128)(2,1)}, bf16[2,4,384,768]{3,...) custom-call(bf16[384,768]{1,0:T(8,128)(2,1)} %refs_0_.1, ...), custom_call_target="tpu_custom_call" | custom-call | tf_op jit(solution)/shard_map/gather_project/pallas_call | solution.py:602
  59.2 0.0 copy-done.6
  59.2 0.0 copy-start.1
  59.2 1.5 copy-done.1
  60.7 0.0 copy-start.2
  60.7 1.5 copy-done.2
  62.3 0.0 copy-start.4
  62.3 21.8 %attend.1 = (bf16[2,640,768]{2,1,0:T(8,128)(2,1)S(1)}, f32[2,6,2,640]{3,2,1,0:T(2,128)S(1)}) custom-call(s32[2,1,640]{2,1,0:T(1,128)S(1)} %broadcast_in_dim.100.seg, bf16[2,640,768]{2,1,0:T(8,128)(2,1)S(1)} %copy-done.1, bf16[2,640,768]{2,1,0:T(8,128)(2,1)S(1)} %copy-done.2, bf16[2,640,768]{2,1,0:T(8,128)(2,1)} %get-tuple-element.62.k, ...), custom_call_target="tpu_custom_call" | custom-call | tf_op jit(solution)/shard_map/attend/pallas_call | solution.py:108
  84.1 0.0 copy-done.4
  84.1 0.0 copy-start
  84.1 1.3 copy-done
  85.4 0.0 copy-start.3
  85.4 0.6 copy-done.3
  86.0 52.5 %middle.1 = (bf16[1280,768]{1,0:T(8,128)(2,1)}, f32[1280,768]{1,0:T(8,128)}, bf16[1280,768]{1,0:T(8,128)(2,1)}, bf16[1280,3072]{1,0:T(8,128)(2,1)}, bf16[1280,30...) custom-call(bf16[1280,768]{1,0:T(8,128)(2,1)} %bitcast.12, ...), custom_call_target="tpu_custom_call" | custom-call | tf_op jit(solution)/shard_map/middle/pallas_call | solution.py:287
  138.6 20.8 %ffn_grads.1 = (bf16[4,768,768]{2,1,0:T(8,128)(2,1)}, bf16[4,768,768]{2,1,0:T(8,128)(2,1)}, bf16[1,768,768]{2,1,0:T(8,128)(2,1)}) custom-call(bf16[1280,768]{1,0:T(8,128)(2,1)} %get-tuple-element.76.hl, bf16[1280,3072]{1,0:T(8,128)(2,1)} %get-tuple-element.77.gu, bf16[1280,3072]{1,0:T(8,128)(2,1)} %get-tuple-element.78.act_lo.act_hi, ...), custom_call_target="tpu_custom_call" | custom-call | tf_op jit(solution)/shard_map/ffn_grads/pallas_call | solution.py:332
  159.4 146.0 %backward.1 = (f32[2,640,768]{2,1,0:T(8,128)}, bf16[15,384,768]{2,1,0:T(8,128)(2,1)}, f32[24,768]{1,0:T(8,128)}) custom-call(s32[2,1,640]{2,1,0:T(1,128)} %copy-done.4, bf16[2,640,768]{2,1,0:T(8,128)(2,1)} %get-tuple-element.60.qw, bf16[2,640,768]{2,1,0:T(8,128)(2,1)} %get-tuple-element.61.qe, bf16[2,640,768]{2,1,0:T(8,128)(2,1)} %get-tuple-element.62.k, ...), custom_call_target="tpu_custom_call" | custom-call | tf_op jit(solution)/shard_map/backward/pallas_call | solution.py:916
  305.3 0.0 copy-start.5
  305.3 9.8 %widen.1 = (f32[384,3072]{1,0:T(8,128)}, f32[1536,768]{1,0:T(8,128)}, f32[384,768]{1,0:T(8,128)}, f32[384,768]{1,0:T(8,128)}, f32[384,768]{1,0:T(8,128)}, /*inde...) custom-call(bf16[15,384,768]{2,1,0:T(8,128)(2,1)} %get-tuple-element.86.g), custom_call_target="tpu_custom_call" | custom-call | tf_op jit(solution)/shard_map/widen/pallas_call | solution.py:665
  315.1 0.0 copy-done.5
  315.1 0.7 dynamic-slice_reduce_fusion
  315.9 0.7 dynamic_slice.7
  316.6 4.3 %copy.48 = f32[2,640,768]{2,1,0:T(8,128)} copy(f32[2,640,768]{2,1,0:T(8,128)} %get-tuple-element.150) | data formatting | bytes 7864320
  (12 shorter events, 0.1 us)
Async XLA Ops:
  3.1 56.0 %copy-start.6 = (s32[2,640]{1,0:T(2,128)S(1)}, s32[2,640]{1,0:T(2,128)}, u32[]{:S(2)}) copy-start(s32[2,640]{1,0:T(2,128)} %param.25) | copy-start | bytes 15364
  59.2 1.5 copy-start.1
  60.7 1.5 copy-start.2
  62.3 21.8 %copy-start.4 = (s32[2,1,640]{2,1,0:T(1,128)}, s32[2,1,640]{2,1,0:T(1,128)S(1)}, u32[]{:S(2)}) copy-start(s32[2,1,640]{2,1,0:T(1,128)S(1)} %broadcast_in_dim.100.seg) | copy-start | bytes 15364
  84.1 1.3 copy-start
  85.4 0.6 copy-start.3
  305.3 9.8 %copy-start.5 = (f32[24,768]{1,0:T(8,128)S(1)}, f32[24,768]{1,0:T(8,128)}, u32[]{:S(2)}) copy-start(f32[24,768]{1,0:T(8,128)} %get-tuple-element.91) | copy-start | bytes 221188
